TPU v7x, 128 devices: a whole 4x4x4 slice. The times are simulated.
128 devices in a mesh: exp: 16 (over y, z_hi, core), row: 8 (over z_lo, x).
Axes of the slice: x: 4, y: 4, z: 4 (z_hi: 2, z_lo: 2; z = z_hi * 2 + z_lo), core: 2. Of those that a mesh axis runs over, the one named last changes fastest.
Arguments:
- exposures: bfloat16 [16, 39, 128, 2048], P('exp', None, 'row'), may hold values from -6 to 6
- fake_flux: float32 [16, 39, 16], P('exp'), may hold values from -24 to 24
- fake_rows: int32 [16], replicated, may hold values from 0 to 127
- fake_cols: int32 [16], replicated, may hold values from 0 to 2047
- kernel_taps: float32 [39, 16], replicated, may hold values from -0.25 to 0.5
- band_offsets: int32 [39], replicated, may hold values from -12 to -4, as said below
- analysis: bfloat16 [8, 39], replicated, may hold values from -1 to 1
- spectral_basis: bfloat16 [39, 8], replicated, may hold values from -2 to 2
- exposure_weights: float32 [16], replicated, may hold values from -4 to 4
Outputs:
- detection_map: float32 [39, 128, 2048], P(None, 'exp', 'row')
Inputs may be any that keep to these rules, and one draw needn't show every extreme that they name: `band_offsets`: each channel's offset lies in a range such that every output pixel reads pixels at most 12 away; some channel has the smallest offset and some the largest.
All inputs are finite; a program needn't handle non-finite values.
Results may differ from a plain program's by a relative error of at most 0.0065.
Values may be sent and summed in bfloat16 or wider, within the bound.
No kernel may reach another device: no remote copies, remote signals or barrier semaphores. Data moves between devices by JAX's collectives and lax.ppermute only.
A program may use at most 128 MiB of HBM per device.

v0:
```python
import jax
import jax.numpy as jnp
from jax import lax
from jax.sharding import PartitionSpec as P

REACH = 12


def band(tap_values, offsets, count_out, count_in, lead):
    outer = lax.broadcasted_iota(jnp.int32, (count_out, count_in), 0)
    inner = lax.broadcasted_iota(jnp.int32, (count_out, count_in), 1)
    distance = inner[None, :, :] - lead - outer[None, :, :] - offsets[:, None, None]
    matrix = jnp.zeros((tap_values.shape[0], count_out, count_in), jnp.float32)
    for tap_index in range(tap_values.shape[1]):
        weight = tap_values[:, tap_index].astype(jnp.float32)[:, None, None]
        matrix = matrix + jnp.where(distance == tap_index, weight, 0.0)
    return matrix.astype(jnp.bfloat16)


def project(resampled, analysis, spectral_basis):
    coefficients = jnp.einsum(
        "kc,echw->ekhw", analysis, resampled, preferred_element_type=jnp.float32
    ).astype(jnp.bfloat16)
    model = jnp.einsum(
        "ck,ekhw->echw", spectral_basis, coefficients, preferred_element_type=jnp.float32
    )
    return (resampled.astype(jnp.float32) - model).astype(jnp.bfloat16)


def body(
    exposures,
    fake_flux,
    fake_rows,
    fake_cols,
    kernel_taps,
    band_offsets,
    analysis,
    spectral_basis,
    exposure_weights,
):
    local_exp, channels, local_rows, width = exposures.shape
    tap_values = kernel_taps.astype(jnp.bfloat16)
    row_start = lax.axis_index("row") * local_rows
    row_ids = row_start + lax.broadcasted_iota(jnp.int32, (local_rows,), 0)
    col_ids = lax.broadcasted_iota(jnp.int32, (width,), 0)
    row_hits = (fake_rows[:, None] == row_ids[None, :]).astype(jnp.float32)
    col_hits = (fake_cols[:, None] == col_ids[None, :]).astype(jnp.float32)
    added = jnp.einsum(
        "ecf,fh,fw->echw", fake_flux, row_hits, col_hits, precision=lax.Precision.HIGHEST
    )
    injected = (exposures.astype(jnp.float32) + added).astype(jnp.bfloat16)
    block = min(512, width)
    column_kernel = band(tap_values, band_offsets, block, block + 2 * REACH, REACH)
    padded = jnp.pad(injected, ((0, 0), (0, 0), (0, 0), (REACH, REACH)))
    pieces = []
    for block_index in range(width // block):
        window = padded[:, :, :, block_index * block : block_index * block + block + 2 * REACH]
        pieces.append(
            jnp.einsum("echj,cwj->echw", window, column_kernel, preferred_element_type=jnp.float32)
        )
    first = jnp.concatenate(pieces, axis=3).astype(jnp.bfloat16)
    columns = lax.all_to_all(first, "row", split_axis=3, concat_axis=2, tiled=True)
    all_rows = columns.shape[2]
    row_kernel = band(tap_values, band_offsets, all_rows, all_rows, 0)
    second = jnp.einsum(
        "cij,ecjw->eciw", row_kernel, columns, preferred_element_type=jnp.float32
    ).astype(jnp.bfloat16)
    residual = project(second, analysis, spectral_basis)
    total_exp = local_exp * lax.axis_size("exp")
    own_weights = lax.dynamic_slice_in_dim(
        exposure_weights, lax.axis_index("exp") * local_exp, local_exp
    )
    values = residual.astype(jnp.float32)
    first_sum = jnp.sum(values, axis=0)
    weighted_sum = jnp.einsum("e,echw->chw", own_weights, values, precision=lax.Precision.HIGHEST)
    square_sum = jnp.sum(values * values, axis=0)
    first_sum, weighted_sum, square_sum = (
        lax.psum_scatter(first_sum, "exp", scatter_dimension=1, tiled=True),
        lax.psum_scatter(weighted_sum, "exp", scatter_dimension=1, tiled=True),
        lax.psum_scatter(square_sum, "exp", scatter_dimension=1, tiled=True),
    )
    mean_level = first_sum / total_exp
    weighted = weighted_sum - mean_level * jnp.sum(exposure_weights)
    spread = square_sum / total_exp - mean_level * mean_level + 1e-05
    return weighted / jnp.sqrt(total_exp * spread)


def solution(mesh):
    return jax.shard_map(
        body,
        mesh=mesh,
        in_specs=(
            P("exp", None, "row", None),
            P("exp", None, None),
            P(),
            P(),
            P(),
            P(),
            P(),
            P(),
            P(),
        ),
        out_specs=P(None, "exp", "row"),
        check_vma=False,
    )
```

profile of v0, /device:TPU:6, one launch (start us, length us, event | category | flops | bytes accessed | tf_op | source)
XLA Modules:
  0.0 530.2 jit_solution(3733225027252749693)
XLA Ops:
  6.5 0.0 copy-start
  6.5 0.1 iota_subtract_fusion
  6.7 0.7 convert_element_type.229
  7.4 0.7 compare_convert_fusion
  8.1 0.0 copy-start.2
  8.1 6.5 %fusion = bf16[1,39,16,2048]{3,1,2,0:T(8,128)(2,1)S(1)} fusion(bf16[1,39,16,2048]{3,2,1,0:T(8,128)(2,1)} %param.9, s32[16]{0:T(128)} %param.12, f32[16,39]{1,0:T(8,128)} %bitcast.168, f32[16,16]{0,1:T(8,128)S(1)} %compare_convert_fusion), kind=kOutput, calls=%fused_computation.37 | convolution fusion | flops 249243392 | bytes 5115392 | tf_op jit(solution)/shard_map/ecf,fh,fw->echw/dot_general | solution.py:48
  14.6 1.7 fusion.45
  16.3 0.0 copy-done.2
  16.3 70.8 %add_convert_fusion = bf16[39,512,536]{1,2,0:T(8,128)(2,1)} fusion(f32[39]{0:T(128)S(1)} %get-tuple-element.12, f32[39]{0:T(128)S(1)} %get-tuple-element.13, f32[39]{0:T(128)S(1)} %get-tuple-element.14, f32[39]{0:T(128)S(1)} %get-tuple-element.15, f32[39]{0:T(128)S(1)} %get-tuple-element.16, f32[39]{0:T(128)S(1)} %get-tuple-element.17, ...), kind=kLoop, calls=%fused_computation.16 | loop fusion | flops 524439552 | bytes 22506076 | tf_op jit(solution)/shard_map/convert_element_type | solution.py:17
  87.1 8.7 %fusion.42 = bf16[1,39,16,512]{3,2,1,0:T(8,128)(2,1)S(1)} fusion(bf16[39,512,536]{1,2,0:T(8,128)(2,1)} %add_convert_fusion, bf16[39,16,536]{2,0,1:T(8,128)(2,1)S(1)} %get-tuple-element.8), kind=kOutput, calls=%fused_computation.90 | convolution fusion | flops 342810624 | bytes 22713600 | tf_op jit(solution)/shard_map/echj,cwj->echw/dot_general | solution.py:59
  95.8 8.9 %fusion.41 = bf16[1,39,16,512]{3,2,1,0:T(8,128)(2,1)S(1)} fusion(bf16[39,512,536]{1,2,0:T(8,128)(2,1)} %add_convert_fusion, bf16[39,16,536]{2,0,1:T(8,128)(2,1)S(1)} %get-tuple-element.9), kind=kOutput, calls=%fused_computation.89 | convolution fusion | flops 342810624 | bytes 22713600 | tf_op jit(solution)/shard_map/echj,cwj->echw/dot_general | solution.py:59
  104.7 8.7 %fusion.40 = bf16[1,39,16,512]{3,2,1,0:T(8,128)(2,1)S(1)} fusion(bf16[39,512,536]{1,2,0:T(8,128)(2,1)} %add_convert_fusion, bf16[39,16,536]{2,0,1:T(8,128)(2,1)S(1)} %get-tuple-element.10), kind=kOutput, calls=%fused_computation.88 | convolution fusion | flops 342810624 | bytes 22713600 | tf_op jit(solution)/shard_map/echj,cwj->echw/dot_general | solution.py:59
  113.4 8.7 %fusion.39 = bf16[1,39,16,512]{3,2,1,0:T(8,128)(2,1)S(1)} fusion(bf16[39,512,536]{1,2,0:T(8,128)(2,1)} %add_convert_fusion, bf16[39,16,536]{2,0,1:T(8,128)(2,1)S(1)} %get-tuple-element.7), kind=kOutput, calls=%fused_computation.87 | convolution fusion | flops 342810624 | bytes 22713600 | tf_op jit(solution)/shard_map/echj,cwj->echw/dot_general | solution.py:59
  122.1 0.3 pad_maximum_fusion
  122.4 10.2 %copy.62 = bf16[1,39,16,2048]{1,2,0,3:T(8,128)(2,1)} copy(bf16[1,39,16,2048]{3,2,1,0:T(8,128)(2,1)S(1)} %pad_maximum_fusion) | data formatting | bytes 5111808 | tf_op jit(solution)/shard_map/concatenate | solution.py:61
  132.6 16.3 %reshape.268 = bf16[8,2,79872]{2,1,0:T(2,128)(2,1)} reshape(bf16[2048,1,16,39]{3,2,1,0:T(8,128)(2,1)} %bitcast.163) | data formatting | bytes 5111808
  149.0 0.0 copy-start.3
  149.0 6.3 %all-to-all-start = ((bf16[8,2,79872]{2,1,0:T(2,128)(2,1)}), bf16[8,2,79872]{2,1,0:T(2,128)(2,1)S(1)}, u32[]{:S(2)}, u32[]{:S(2)}) async-start(bf16[8,2,79872]{2,1,0:T(2,128)(2,1)} %reshape.268), calls=%async_computation | async-start | bytes 5111808 | tf_op jit(solution)/shard_map/all_to_all | solution.py:62
  155.2 0.0 reduce-scatter.4.cloned.1.call-start
  155.2 0.0 copy-done.3
  155.2 0.6 dynamic_slice.3
  155.8 34.6 %all-to-all-done = bf16[8,2,79872]{2,1,0:T(2,128)(2,1)S(1)} async-done(((bf16[8,2,79872]{2,1,0:T(2,128)(2,1)}), bf16[8,2,79872]{2,1,0:T(2,128)(2,1)S(1)}, u32[]{:S(2)}, u32[]{:S(2)}) %all-to-all-start) | async-done | bytes 2555936 | tf_op jit(solution)/shard_map/all_to_all | solution.py:62
  190.4 24.8 %reshape.269 = bf16[2048,1,16,39]{3,2,1,0:T(8,128)(2,1)} reshape(bf16[8,2,79872]{2,1,0:T(2,128)(2,1)S(1)} %all-to-all-done) | data formatting | bytes 5111808
  215.2 9.8 %copy.73 = bf16[1,39,16,8,256]{4,3,2,1,0:T(8,128)(2,1)S(1)} copy(bf16[1,39,16,8,256]{1,2,4,3,0:T(8,128)(2,1)} %bitcast.164) | data formatting | bytes 5111808 | tf_op jit(solution)/shard_map/all_to_all | solution.py:62
  225.0 0.8 copy.64
  225.8 6.2 %convolution_convert_fusion = bf16[39,256,128]{2,1,0:T(8,128)(2,1)} fusion(bf16[39,128,256]{2,1,0:T(8,128)(2,1)S(1)} %bitcast.167, f32[39]{0:T(128)S(1)} %get-tuple-element.12, f32[39]{0:T(128)S(1)} %get-tuple-element.13, f32[39]{0:T(128)S(1)} %get-tuple-element.14, f32[39]{0:T(128)S(1)} %get-tuple-element.15, f32[39]{0:T(128)S(1)} %get-tuple-element.16, ...), kind=kOutput, calls=%fused_computation.46 | convolution fusion | flops 359743488 | bytes 5179996 | tf_op jit(solution)/shard_map/cij,ecjw->eciw/dot_general | solution.py:65
  232.0 3.8 copy.66
  235.8 0.0 copy-done
  235.8 0.0 copy-done.1
  235.8 3.5 fusion.44
  239.3 6.2 %copy.67 = f32[128,256,39]{0,1,2:T(8,128)} copy(f32[128,256,39]{1,2,0:T(8,128)} %fusion.44) | data formatting | bytes 10223616 | tf_op jit(solution)/shard_map/ck,ekhw->echw/dot_general | solution.py:24
  245.5 7.3 %fusion.1 = (f32[39,128,256]{1,2,0:T(8,128)}, bf16[1,39,128,256]{2,3,1,0:T(8,128)(2,1)S(1)}) fusion(f32[]{:T(128)} %bitcast, f32[128,256,39]{0,1,2:T(8,128)} %copy.67, bf16[39,256,128]{2,1,0:T(8,128)(2,1)} %convolution_convert_fusion), kind=kLoop, calls=%fused_computation.38 | loop fusion | flops 6389760 | bytes 15335428 | tf_op jit(solution)/shard_map/e,echw->chw/dot_general | solution.py:75
  252.8 6.1 %copy.68 = f32[39,128,256]{2,0,1:T(8,128)} copy(f32[39,128,256]{1,2,0:T(8,128)} %get-tuple-element.5) | data formatting | bytes 10223616 | tf_op jit(solution)/shard_map/e,echw->chw/dot_general | solution.py:75
  258.9 0.0 reduce-scatter.4.cloned.1.call-update
  258.9 0.0 reduce-scatter.8.cloned.1.call-start
  259.0 3.0 fusion.2
  262.0 6.1 %copy.70 = f32[39,128,256]{2,0,1:T(8,128)} copy(f32[39,128,256]{1,2,0:T(8,128)} %fusion.2) | data formatting | bytes 10223616 | tf_op jit(solution)/shard_map/reduce_sum | solution.py:76
  268.1 0.0 reduce-scatter.8.cloned.1.call-update
  268.1 0.0 reduce-scatter.6.cloned.1.call-start
  268.2 2.8 convert_bitcast_fusion
  271.0 6.3 %copy.69 = f32[39,128,256]{2,0,1:T(8,128)} copy(f32[39,128,256]{1,2,0:T(8,128)} %convert_bitcast_fusion) | data formatting | bytes 10223616 | tf_op jit(solution)/shard_map/reduce_sum | solution.py:74
  277.3 0.0 reduce-scatter.6.cloned.1.call-update
  277.4 0.6 reduce_sum.16
  278.6 67.2 %reduce-scatter.4.cloned.1.call-done = f32[39,8,256]{2,0,1:T(8,128)} async-done(((f32[39,128,256]{2,0,1:T(8,128)}), f32[39,8,256]{2,0,1:T(8,128)}) %reduce-scatter.4.cloned.1.call-update) | async-done | bytes 319504 | tf_op jit(solution)/shard_map/reduce_scatter | solution.py:79
  345.8 87.9 %reduce-scatter.8.cloned.1.call-done = f32[39,8,256]{2,0,1:T(8,128)} async-done(((f32[39,128,256]{2,0,1:T(8,128)}), f32[39,8,256]{2,0,1:T(8,128)}) %reduce-scatter.8.cloned.1.call-update) | async-done | bytes 319504 | tf_op jit(solution)/shard_map/reduce_scatter | solution.py:80
  433.7 87.9 %reduce-scatter.6.cloned.1.call-done = f32[39,8,256]{2,0,1:T(8,128)} async-done(((f32[39,128,256]{2,0,1:T(8,128)}), f32[39,8,256]{2,0,1:T(8,128)}) %reduce-scatter.6.cloned.1.call-update) | async-done | bytes 319504 | tf_op jit(solution)/shard_map/reduce_scatter | solution.py:78
  521.6 1.3 rsqrt_multiply_fusion
  522.9 0.8 copy.71
  (4 shorter events, 0.0 us)
Async XLA Ops:
  6.5 229.2 %copy-start = (bf16[39,8]{0,1:T(8,128)(2,1)S(1)}, bf16[39,8]{0,1:T(8,128)(2,1)}, u32[]{:S(2)}) copy-start(bf16[39,8]{0,1:T(8,128)(2,1)} %param.16) | copy-start | bytes 1876
  8.1 8.2 %copy-start.2 = (s32[39]{0:T(128)S(1)}, s32[39]{0:T(128)}, u32[]{:S(2)}) copy-start(s32[39]{0:T(128)} %param.14) | copy-start | bytes 472
  149.0 6.3 %copy-start.3 = (f32[16]{0:T(128)S(1)}, f32[16]{0:T(128)}, u32[]{:S(2)}) copy-start(f32[16]{0:T(128)} %param.17) | copy-start | bytes 196
  149.0 41.4 %all-to-all-start = ((bf16[8,2,79872]{2,1,0:T(2,128)(2,1)}), bf16[8,2,79872]{2,1,0:T(2,128)(2,1)S(1)}, u32[]{:S(2)}, u32[]{:S(2)}) async-start(bf16[8,2,79872]{2,1,0:T(2,128)(2,1)} %reshape.268), calls=%async_computation | async-start | bytes 5111808 | tf_op jit(solution)/shard_map/all_to_all | solution.py:62
  155.2 190.6 %reduce-scatter.4.cloned.1.call-start = ((), (), s32[]{:S(2)}) async-start(), calls=%async_computation.4 | async-start | bytes 5570560 | tf_op jit(solution)/shard_map/reduce_scatter | solution.py:79
  232.0 3.8 copy-start.1
  258.9 174.8 %reduce-scatter.8.cloned.1.call-start = ((), (), s32[]{:S(2)}) async-start(), calls=%async_computation.6 | async-start | bytes 5570560 | tf_op jit(solution)/shard_map/reduce_scatter | solution.py:80
  268.1 253.4 %reduce-scatter.6.cloned.1.call-start = ((), (), s32[]{:S(2)}) async-start(), calls=%async_computation.5 | async-start | bytes 5570560 | tf_op jit(solution)/shard_map/reduce_scatter | solution.py:78
Sparse Core Ops, SparseCore 0:
  259.1 86.7 reduce-scatter.3
  349.9 83.7 reduce-scatter.7
  437.8 83.7 reduce-scatter.5
where the time goes:
time: 531 us; the launch traced here: 530 us
  waiting for transfers between devices  278 us (52%)
  local copies, waits for them, and re-layouts  93.6 us (18%)
  other arithmetic  87.6 us (16%)
  matrix products  51.2 us (10%)
  between operations  13.9 us (3%)
  starting transfers between devices  6.35 us (1%)
    reduce_scatter x1, waiting for transfers between devices, body(): lax.psum_scatter(square_sum, 'exp', scatter_dimension=1, tiled=True)  87.9 us
    reduce_scatter x1, waiting for transfers between devices, body(): lax.psum_scatter(first_sum, 'exp', scatter_dimension=1, tiled=True)  87.9 us
    convert_element_type x1, other arithmetic, band(): return matrix.astype(jnp.bfloat16)  70.8 us
    reduce_scatter x1, waiting for transfers between devices, body(): lax.psum_scatter(weighted_sum, 'exp', scatter_dimension=1, tiled=True)  67.2 us
    unnamed x10, local copies, waits for them, and re-layouts  41.1 us
    dot_general x4, matrix products, body(): jnp.einsum('echj,cwj->echw', window, column_kernel, preferred_element_typ...  35 us
    all_to_all x1, waiting for transfers between devices, body(): lax.all_to_all(first, 'row', split_axis=3, concat_axis=2, tiled=True)  34.6 us
  transfers between devices with their start and end apart: 4, of which 4 were waited for; matrix products, arithmetic and copies ran while one was open for 4% of the time, Pallas kernels for 0%

commit v1 on v0

v1 whole, which is shorter than its diff:
```python
import jax
import jax.numpy as jnp
from jax import lax
from jax.experimental import pallas as pl
from jax.experimental.pallas import tpu as pltpu
from jax.sharding import PartitionSpec as P

BLOCK = 256
HALF = 128
NEAR = 64
VMEM = pl.BlockSpec(memory_space=pltpu.VMEM)
SMEM = pl.BlockSpec(memory_space=pltpu.SMEM)


def circulant(taps_ref, offsets_ref, channel, sign):
    lane = lax.broadcasted_iota(jnp.int32, (8, HALF), 1)
    signed = jnp.where(lane < NEAR, lane, lane - HALF)
    place = sign * signed - offsets_ref[channel]
    values = jnp.zeros((8, HALF), jnp.float32)
    for tap_index in range(taps_ref.shape[1]):
        values = jnp.where(place == tap_index, taps_ref[channel, tap_index], values)
    rows = jnp.concatenate([values] * (HALF // 8), axis=0)
    return pltpu.roll(rows, 0, 1, stride=1, stride_axis=0)


def distances():
    inner = lax.broadcasted_iota(jnp.int32, (HALF, HALF), 0)
    outer = lax.broadcasted_iota(jnp.int32, (HALF, HALF), 1)
    return outer - inner


def columns_kernel(
    rows_ref, cols_ref, offsets_ref, taps_ref, flux_ref, frames_ref, sent_ref, held_ref
):
    channels, local_rows, width = frames_ref.shape
    pieces = width // BLOCK
    row_start = lax.axis_index("row") * local_rows
    held_ref[...] = frames_ref[...]
    count = rows_ref.shape[0]

    def inject(which, carry):
        local = rows_ref[which] - row_start
        column = cols_ref[which]
        first = jnp.int32(1)
        for other in range(count):
            same = (rows_ref[other] == rows_ref[which]) & (cols_ref[other] == column)
            first = jnp.where(same & (other < which), 0, first)

        @pl.when((local >= 0) & (local < local_rows) & (first == 1))
        def _():
            start = pl.multiple_of((column // HALF) * HALF, HALF)
            row_ids = lax.broadcasted_iota(jnp.int32, (local_rows, HALF), 0)
            col_ids = lax.broadcasted_iota(jnp.int32, (local_rows, HALF), 1)
            hit = (row_ids == local) & (col_ids == column - start)

            def one(channel, inner):
                total = jnp.float32(0.0)
                for other in range(count):
                    same = (rows_ref[other] == rows_ref[which]) & (cols_ref[other] == column)
                    total = total + jnp.where(same, flux_ref[0, channel, other], 0.0)
                tile = held_ref[channel, :, pl.ds(start, HALF)].astype(jnp.float32)
                held_ref[channel, :, pl.ds(start, HALF)] = jnp.where(
                    hit, tile + total, tile
                ).astype(jnp.bfloat16)
                return inner

            lax.fori_loop(0, channels, one, 0)

        return carry

    lax.fori_loop(0, count, inject, 0)
    gap = distances()
    empty = jnp.zeros((HALF, HALF), jnp.bfloat16)
    edge = jnp.zeros((local_rows, HALF), jnp.bfloat16)

    def resample(channel, carry):
        ring = circulant(taps_ref, offsets_ref, channel, -1)
        near = jnp.where(jnp.abs(gap) < NEAR, ring, 0.0).astype(jnp.bfloat16)
        after = jnp.where(gap >= NEAR, ring, 0.0).astype(jnp.bfloat16)
        before = jnp.where(gap <= -NEAR, ring, 0.0).astype(jnp.bfloat16)
        weights = jnp.concatenate(
            [
                jnp.concatenate([near, before], axis=1),
                jnp.concatenate([after, near], axis=1),
                jnp.concatenate([empty, after], axis=1),
                jnp.concatenate([before, empty], axis=1),
            ],
            axis=0,
        )
        values = held_ref[channel]
        lines = []
        for piece in range(pieces):
            start = piece * BLOCK
            follow = values[:, start + BLOCK : start + BLOCK + HALF] if piece < pieces - 1 else edge
            lead = values[:, start - HALF : start] if piece > 0 else edge
            lines.append(
                jnp.concatenate([values[:, start : start + BLOCK], follow, lead], axis=1)
            )
        result = jnp.dot(
            jnp.concatenate(lines, axis=0), weights, preferred_element_type=jnp.float32
        ).astype(jnp.bfloat16)
        for piece in range(pieces):
            sent_ref[piece, channel] = result[piece * local_rows : (piece + 1) * local_rows]
        return carry

    lax.fori_loop(0, channels, resample, 0)


def rows_kernel(
    offsets_ref, taps_ref, analysis_ref, basis_ref, columns_ref, sent_ref, resampled_ref
):
    parts, channels, part_rows, width = columns_ref.shape
    rows = parts * part_rows
    gap = distances()

    def resample(channel, carry):
        ring = circulant(taps_ref, offsets_ref, channel, 1)
        near = jnp.where(jnp.abs(gap) < NEAR, ring, 0.0).astype(jnp.bfloat16)
        values = columns_ref[:, channel].reshape(rows, width)
        resampled_ref[channel] = jnp.dot(
            near, values, preferred_element_type=jnp.float32
        ).astype(jnp.bfloat16)
        return carry

    lax.fori_loop(0, channels, resample, 0)
    group = basis_ref.shape[0] // channels
    owned = sent_ref.shape[2]

    for index in range(rows // group):
        block = resampled_ref[:, index * group : (index + 1) * group, :].reshape(
            channels * group, width
        )
        coefficients = jnp.dot(
            analysis_ref[...], block, preferred_element_type=jnp.float32
        ).astype(jnp.bfloat16)
        model = jnp.dot(basis_ref[...], coefficients, preferred_element_type=jnp.float32)
        residual = (block.astype(jnp.float32) - model).reshape(
            channels, group // owned, owned, width
        )
        for part in range(group // owned):
            sent_ref[index * (group // owned) + part] = residual[:, part].astype(jnp.bfloat16)


def combine_kernel(weights_ref, values_ref, map_ref):
    total, channels = values_ref.shape[0], values_ref.shape[1]

    def one(channel, carry):
        mean_level = values_ref[0, channel].astype(jnp.float32)
        for index in range(1, total):
            mean_level = mean_level + values_ref[index, channel].astype(jnp.float32)
        mean_level = mean_level / total
        spread = jnp.zeros_like(mean_level)
        weighted = jnp.zeros_like(mean_level)
        for index in range(total):
            deviation = values_ref[index, channel].astype(jnp.float32) - mean_level
            spread = spread + deviation * deviation
            weighted = weighted + weights_ref[index] * deviation
        spread = spread / total + 1e-05
        map_ref[channel] = weighted / jnp.sqrt(total * spread)
        return carry

    lax.fori_loop(0, channels, one, 0)


def body(
    exposures,
    fake_flux,
    fake_rows,
    fake_cols,
    kernel_taps,
    band_offsets,
    analysis,
    spectral_basis,
    exposure_weights,
):
    _, channels, local_rows, width = exposures.shape
    row_parts = lax.axis_size("row")
    exp_parts = lax.axis_size("exp")
    owned_rows = local_rows * row_parts // exp_parts
    taps = kernel_taps.astype(jnp.bfloat16).astype(jnp.float32)
    first = pl.pallas_call(
        columns_kernel,
        out_shape=jax.ShapeDtypeStruct((row_parts, channels, local_rows, BLOCK), jnp.bfloat16),
        in_specs=[SMEM, SMEM, SMEM, SMEM, SMEM, VMEM],
        out_specs=VMEM,
        scratch_shapes=[pltpu.VMEM((channels, local_rows, width), jnp.bfloat16)],
        name="columns",
    )(fake_rows, fake_cols, band_offsets, taps, fake_flux, exposures[0])
    columns = lax.all_to_all(first, "row", split_axis=0, concat_axis=0, tiled=True)
    same = jnp.eye(local_rows, dtype=jnp.bfloat16)
    residual = pl.pallas_call(
        rows_kernel,
        out_shape=jax.ShapeDtypeStruct((exp_parts, channels, owned_rows, BLOCK), jnp.bfloat16),
        in_specs=[SMEM, SMEM, VMEM, VMEM, VMEM],
        out_specs=VMEM,
        scratch_shapes=[pltpu.VMEM((channels, local_rows * row_parts, BLOCK), jnp.bfloat16)],
        name="rows",
    )(band_offsets, taps, jnp.kron(analysis, same), jnp.kron(spectral_basis, same), columns)
    gathered = lax.all_to_all(residual, "exp", split_axis=0, concat_axis=0, tiled=True)
    return pl.pallas_call(
        combine_kernel,
        out_shape=jax.ShapeDtypeStruct((channels, owned_rows, BLOCK), jnp.float32),
        in_specs=[SMEM, VMEM],
        out_specs=VMEM,
        name="combine",
    )(exposure_weights, gathered)


def solution(mesh):
    return jax.shard_map(
        body,
        mesh=mesh,
        in_specs=(
            P("exp", None, "row", None),
            P("exp", None, None),
            P(),
            P(),
            P(),
            P(),
            P(),
            P(),
            P(),
        ),
        out_specs=P(None, "exp", "row"),
        check_vma=False,
    )
```

time: 531 us -> 128 us (0.24)
  waiting for transfers between devices: 278 us -> 26.7 us
  other arithmetic: 87.6 us -> 3.09 us
  local copies, waits for them, and re-layouts: 93.6 us -> 9.68 us
  matrix products: 51.2 us -> 0 us
  blocking collectives: 0 us -> 41.8 us
  Pallas kernels: 0 us -> 39.3 us
  between operations: 13.9 us -> 0.02 us
    reduce_scatter x3 -> x0, waiting for transfers between devices: 243 us -> none  [the longest x1 87.9 us: body(): lax.psum_scatter(square_sum, 'exp', scatter_dimension=1, tiled=True)]
    convert_element_type x3 -> x2, other arithmetic: 71.5 us -> 0.62 us  [the longest x1 0.61 us: body(): taps = kernel_taps.astype(jnp.bfloat16).astype(jnp.float32)]
    dot_general x7 -> x0, matrix products: 51.2 us -> none  [the longest x4 35 us: body(): jnp.einsum('echj,cwj->echw', window, column_kernel, preferred_element_typ...]
    all_to_all x0 -> x1, blocking collectives: none -> 41.8 us  [body(): lax.all_to_all(residual, 'exp', split_axis=0, concat_axis=0, tiled=True)]
    pallas_call x0 -> x3, Pallas kernels: none -> 39.3 us  [the longest x1 20.2 us: body(): pl.pallas_call(columns_kernel, out_shape=jax.ShapeDtypeStruct((row_parts,...]
    unnamed x10, local copies, waits for them, and re-layouts: 41.1 us -> 3.89 us
    reduce_sum x2 -> x0, local copies, waits for them, and re-layouts: 12.5 us -> none  [the longest x1 6.33 us: body(): first_sum = jnp.sum(values, axis=0)]
    dot_general x2 -> x0, local copies, waits for them, and re-layouts: 12.3 us -> none  [the longest x1 6.21 us: project(): jnp.einsum('ck,ekhw->echw', spectral_basis, coefficients, preferred_eleme...]
  transfers between devices with their start and end apart: 4 -> 1, of which waited for: 4 -> 1; matrix products, arithmetic and copies ran while one was open for 4% -> 7% of each run, Pallas kernels for 0% -> 0%
where the time goes in v1:
time: 128 us; the launch traced here: 127 us
  blocking collectives  41.8 us (33%)
  Pallas kernels  39.3 us (31%)
  waiting for transfers between devices  26.7 us (21%)
  local copies, waits for them, and re-layouts  9.68 us (8%)
  starting transfers between devices  5.99 us (5%)
  other arithmetic  3.09 us (2%)
    all_to_all x1, blocking collectives, body(): lax.all_to_all(residual, 'exp', split_axis=0, concat_axis=0, tiled=True)  41.8 us
    all_to_all x1, waiting for transfers between devices, body(): lax.all_to_all(first, 'row', split_axis=0, concat_axis=0, tiled=True)  26.7 us
    pallas_call x1, Pallas kernels, body(): pl.pallas_call(columns_kernel, out_shape=jax.ShapeDtypeStruct((row_parts,...  20.2 us
    pallas_call x1, Pallas kernels, body(): pl.pallas_call(rows_kernel, out_shape=jax.ShapeDtypeStruct((exp_parts, ch...  14.1 us
    all_to_all x1, starting transfers between devices, body(): lax.all_to_all(first, 'row', split_axis=0, concat_axis=0, tiled=True)  5.99 us
    pallas_call x1, Pallas kernels, body(): pl.pallas_call(combine_kernel, out_shape=jax.ShapeDtypeStruct((channels,...  4.94 us
    unnamed x10, local copies, waits for them, and re-layouts  3.89 us
    mul x2, local copies, waits for them, and re-layouts, body(): jnp.kron(analysis, same)  2.96 us
  transfers between devices with their start and end apart: 1, of which 1 were waited for; matrix products, arithmetic and copies ran while one was open for 7% of the time, Pallas kernels for 0%

profile of v1, /device:TPU:6, one launch (start us, length us, event | category | flops | bytes accessed | tf_op | source)
XLA Modules:
  0.0 126.6 jit_solution(4264860740343283139)
XLA Ops:
  0.0 0.8 copy.13
  0.8 0.6 convert_element_type.21.taps_ref
  1.4 1.4 %copy.17.flux_ref = f32[1,39,16]{2,1,0:T(8,128)} copy(f32[1,39,16]{1,2,0:T(8,128)} %param.10) | data formatting | bytes 4992 | tf_op args[1]
  2.8 20.2 %columns.1 = bf16[8,39,16,256]{3,2,1,0:T(8,128)(2,1)} custom-call(s32[16]{0:T(128)} %rows_ref.1, s32[16]{0:T(128)} %cols_ref.1, s32[39]{0:T(128)} %offsets_ref.3, f32[39,16]{1,0:T(8,128)} %convert_element_type.21.taps_ref, f32[1,39,16]{2,1,0:T(8,128)} %copy.17.flux_ref, bf16[39,16,2048]{2,1,0:T(8,128)(2,1)} %bitcast.7), custom_call_target="tpu_custom_call" | custom-call | tf_op jit(solution)/shard_map/columns/pallas_call | solution.py:181
  23.0 0.0 copy-start.1
  23.0 6.0 %all-to-all-start = ((bf16[8,39,16,256]{3,2,1,0:T(8,128)(2,1)}), bf16[8,39,16,256]{3,2,1,0:T(8,128)(2,1)S(1)}, u32[]{:S(2)}, u32[]{:S(2)}) async-start(bf16[8,39,16,256]{3,2,1,0:T(8,128)(2,1)} %columns.1), calls=%async_computation | async-start | bytes 5111808 | tf_op jit(solution)/shard_map/all_to_all | solution.py:189
  29.0 0.1 copy.15
  29.1 0.0 copy-done.1
  29.1 0.1 copy.14
  29.2 0.0 copy-start.2
  29.2 1.2 broadcast_multiply_fusion.1
  30.5 2.1 %mul.51 = bf16[128,624]{0,1:T(8,128)(2,1)S(1)} reshape(bf16[8,16,39,16]{1,0,3,2:T(8,128)(2,1)} %broadcast_multiply_fusion.1) | data formatting | bytes 319488 | tf_op jit(solution)/shard_map/jit(kron)/mul | solution.py:198
  32.6 0.8 copy.18.analysis_ref
  33.4 0.0 copy-done.2
  33.4 0.1 copy.16
  33.5 1.2 broadcast_multiply_fusion
  34.8 2.7 %mul.55.basis_ref = bf16[624,128]{1,0:T(8,128)(2,1)} reshape(bf16[39,16,8,16]{3,2,1,0:T(8,128)(2,1)} %broadcast_multiply_fusion) | data formatting | bytes 319488 | tf_op jit(solution)/shard_map/jit(kron)/mul | solution.py:198
  37.5 26.7 %all-to-all-done.columns_ref = bf16[8,39,16,256]{3,2,1,0:T(8,128)(2,1)S(1)} async-done(((bf16[8,39,16,256]{3,2,1,0:T(8,128)(2,1)}), bf16[8,39,16,256]{3,2,1,0:T(8,128)(2,1)S(1)}, u32[]{:S(2)}, u32[]{:S(2)}) %all-to-all-start) | async-done | bytes 2555936 | tf_op jit(solution)/shard_map/all_to_all | solution.py:189
  64.2 0.0 copy-start
  64.2 1.5 %copy-done = bf16[8,39,16,256]{3,2,1,0:T(8,128)(2,1)} copy-done((bf16[8,39,16,256]{3,2,1,0:T(8,128)(2,1)}, bf16[8,39,16,256]{3,2,1,0:T(8,128)(2,1)S(1)}, u32[]{:S(2)}) %copy-start) | copy-done | bytes 2555928
  65.7 14.1 %rows.1 = bf16[16,39,8,256]{3,2,1,0:T(8,128)(2,1)} custom-call(s32[39]{0:T(128)} %offsets_ref.3, f32[39,16]{1,0:T(8,128)} %convert_element_type.21.taps_ref, bf16[128,624]{1,0:T(8,128)(2,1)} %copy.18.analysis_ref, bf16[624,128]{1,0:T(8,128)(2,1)} %mul.55.basis_ref, bf16[8,39,16,256]{3,2,1,0:T(8,128)(2,1)} %copy-done), custom_call_target="tpu_custom_call" | custom-call | tf_op jit(solution)/shard_map/rows/pallas_call | solution.py:191
  79.9 41.8 %all_to_all.10.values_ref = bf16[16,39,8,256]{3,2,1,0:T(8,128)(2,1)} all-to-all(bf16[16,39,8,256]{3,2,1,0:T(8,128)(2,1)} %rows.1), channel_id=1, replica_groups=mesh['exp'=16,'row'=8] {'exp'}, dimensions={0} | all-to-all | bytes 5111808 | tf_op jit(solution)/shard_map/all_to_all | solution.py:199
  121.6 4.9 %combine.1 = f32[39,8,256]{2,1,0:T(8,128)} custom-call(f32[16]{0:T(128)} %weights_ref.1, bf16[16,39,8,256]{3,2,1,0:T(8,128)(2,1)} %all_to_all.10.values_ref), custom_call_target="tpu_custom_call" | custom-call | tf_op jit(solution)/shard_map/combine/pallas_call | solution.py:200
  (1 shorter events, 0.0 us)
Async XLA Ops:
  23.0 6.1 %copy-start.1 = (bf16[8,39]{1,0:T(8,128)(2,1)S(1)}, bf16[8,39]{1,0:T(8,128)(2,1)}, u32[]{:S(2)}) copy-start(bf16[8,39]{1,0:T(8,128)(2,1)} %param.15) | copy-start | bytes 1876
  23.0 41.2 %all-to-all-start = ((bf16[8,39,16,256]{3,2,1,0:T(8,128)(2,1)}), bf16[8,39,16,256]{3,2,1,0:T(8,128)(2,1)S(1)}, u32[]{:S(2)}, u32[]{:S(2)}) async-start(bf16[8,39,16,256]{3,2,1,0:T(8,128)(2,1)} %columns.1), calls=%async_computation | async-start | bytes 5111808 | tf_op jit(solution)/shard_map/all_to_all | solution.py:189
  29.2 4.2 %copy-start.2 = (bf16[39,8]{0,1:T(8,128)(2,1)S(1)}, bf16[39,8]{0,1:T(8,128)(2,1)}, u32[]{:S(2)}) copy-start(bf16[39,8]{0,1:T(8,128)(2,1)} %param.16) | copy-start | bytes 1876
  64.2 1.5 %copy-start = (bf16[8,39,16,256]{3,2,1,0:T(8,128)(2,1)}, bf16[8,39,16,256]{3,2,1,0:T(8,128)(2,1)S(1)}, u32[]{:S(2)}) copy-start(bf16[8,39,16,256]{3,2,1,0:T(8,128)(2,1)S(1)} %all-to-all-done.columns_ref) | copy-start | bytes 7667716

commit v2 on v0

v2 whole, which is shorter than its diff:
```python
import functools

import jax
import jax.numpy as jnp
from jax import lax
from jax.experimental import pallas as pl
from jax.experimental.pallas import tpu as pltpu
from jax.sharding import PartitionSpec as P


LANES = 128
NEAR = 64
GROUPS = 3
RING = 4
GRANT = 20 * 2**20
VMEM = pl.BlockSpec(memory_space=pltpu.VMEM)
SMEM = pl.BlockSpec(memory_space=pltpu.SMEM)
ANY = pl.BlockSpec(memory_space=pl.ANY)
HBM = pl.BlockSpec(memory_space=pltpu.HBM)


def circulant(taps_ref, offsets_ref, channel, sign):
    lane = lax.broadcasted_iota(jnp.int32, (8, LANES), 1)
    signed = jnp.where(lane < NEAR, lane, lane - LANES)
    place = sign * signed - offsets_ref[channel]
    values = jnp.zeros((8, LANES), jnp.float32)
    for tap_index in range(taps_ref.shape[0]):
        values = jnp.where(place == tap_index, taps_ref[tap_index, channel], values)
    rows = jnp.concatenate([values] * (LANES // 8), axis=0)
    return pltpu.roll(rows, 0, 1, stride=1, stride_axis=0)


def partner(me, step, sign):
    return (me // RING ^ step // RING) * RING + (me + sign * step) % RING


def gaps():
    inner = lax.broadcasted_iota(jnp.int32, (LANES, LANES), 0)
    outer = lax.broadcasted_iota(jnp.int32, (LANES, LANES), 1)
    return jnp.abs(outer - inner)


def inject(rows_ref, cols_ref, flux_ref, held_ref, first_channel, channels):
    local_rows = held_ref.shape[1]
    row_start = lax.axis_index("row") * local_rows
    count = rows_ref.shape[0]

    def one(which, carry):
        row, column = rows_ref[which], cols_ref[which]
        local = row - row_start

        @pl.when((local >= 0) & (local < local_rows))
        def _():
            def look(other, counts):
                same = (rows_ref[other] == row) & (cols_ref[other] == column)
                return (
                    counts[0] + jnp.where(same & (other < which), 1, 0),
                    counts[1] + jnp.where(same & (other > which), 1, 0),
                )

            earlier, later = lax.fori_loop(0, count, look, (jnp.int32(0), jnp.int32(0)))
            start = pl.multiple_of((column // LANES) * LANES, LANES)
            row_ids = lax.broadcasted_iota(jnp.int32, (local_rows, LANES), 0)
            col_ids = lax.broadcasted_iota(jnp.int32, (local_rows, LANES), 1)
            hit = (row_ids == local) & (col_ids == column - start)

            def add(channel, total):
                tile = held_ref[channel, :, pl.ds(start, LANES)].astype(jnp.float32)
                held_ref[channel, :, pl.ds(start, LANES)] = jnp.where(
                    hit, tile + total, tile
                ).astype(jnp.bfloat16)

            @pl.when((earlier == 0) & (later == 0))
            def _():
                for index in range(channels):
                    channel = first_channel + index
                    add(channel, flux_ref[0, which, channel])

            @pl.when((earlier == 0) & (later > 0))
            def _():
                def shared(index, inner):
                    channel = first_channel + index

                    def gather(other, total):
                        same = (rows_ref[other] == row) & (cols_ref[other] == column)
                        return total + jnp.where(same, flux_ref[0, other, channel], 0.0)

                    add(channel, lax.fori_loop(0, count, gather, jnp.float32(0.0)))
                    return inner

                lax.fori_loop(0, channels, shared, 0)

        return carry

    lax.fori_loop(0, count, one, 0)


def columns_kernel(half, count, rows_ref, cols_ref, offsets_ref, taps_ref, flux_ref, frames_ref, *refs):
    sent_refs, (held_ref, done_ref, in_sems, out_sems) = refs[:count], refs[count:]
    channels, local_rows, width = held_ref.shape
    size = channels // GROUPS
    blocks = width // LANES

    def load(group):
        span = pl.ds(group * size, size)
        return pltpu.make_async_copy(frames_ref.at[span], held_ref.at[span], in_sems.at[group])

    def saves(group):
        span = pl.ds(group * size, size)
        if count == 1:
            pairs = [(done_ref.at[:, span], sent_refs[0].at[:, span])]
        else:
            me = lax.axis_index("row")
            pairs = [
                (done_ref.at[partner(me, step, 1), span], sent_refs[step].at[span])
                for step in range(count)
            ]
        return [
            pltpu.make_async_copy(source, target, out_sems.at[group, step])
            for step, (source, target) in enumerate(pairs)
        ]

    for group in range(GROUPS):
        load(group).start()
    gap = gaps()
    lane = lax.broadcasted_iota(jnp.int32, (local_rows, LANES), 1)
    edge = jnp.zeros((local_rows, LANES), jnp.bfloat16)

    def work(group, carry):
        load(group).wait()
        inject(rows_ref, cols_ref, flux_ref, held_ref, group * size, size)
        for index in range(size):
            channel = group * size + index
            ring = circulant(taps_ref, offsets_ref, channel, -1)
            weights = jnp.concatenate(
                [
                    jnp.where(gap < NEAR, ring, 0.0).astype(jnp.bfloat16),
                    jnp.where(gap >= NEAR, ring, 0.0).astype(jnp.bfloat16),
                ],
                axis=0,
            )
            lines = []
            for block in range(half, blocks, 2):
                start = block * LANES
                here = held_ref[channel, :, start : start + LANES]
                after = held_ref[channel, :, start + LANES : start + 2 * LANES] if block < blocks - 1 else edge
                before = held_ref[channel, :, start - LANES : start] if block > 0 else edge
                lines.append(
                    jnp.concatenate([here, jnp.where(lane < NEAR, after, before)], axis=1)
                )
            result = jnp.dot(
                jnp.concatenate(lines, axis=0), weights, preferred_element_type=jnp.float32
            ).astype(jnp.bfloat16)
            for piece in range(blocks // 2):
                done_ref[piece, channel] = result[piece * local_rows : (piece + 1) * local_rows]
        for copy in saves(group):
            copy.start()
        return carry

    lax.fori_loop(0, GROUPS, work, 0)
    for group in range(GROUPS):
        for copy in saves(group):
            copy.wait()


def prepare_kernel(offsets_ref, taps_ref, analysis_ref, basis_ref, band_ref, wide_ref, tall_ref):
    channels = band_ref.shape[0]
    size = channels // GROUPS
    gap = gaps()

    def work(group, carry):
        for index in range(size):
            channel = group * size + index
            ring = circulant(taps_ref, offsets_ref, channel, 1)
            band_ref[channel] = jnp.where(gap < NEAR, ring, 0.0).astype(jnp.bfloat16)
        return carry

    lax.fori_loop(0, GROUPS, work, 0)
    rank = analysis_ref.shape[0]
    short, long = wide_ref.shape
    rows = short // rank

    def onehot(shape, dim):
        left = lax.broadcasted_iota(jnp.int32, shape, dim) // rows
        return (left == lax.broadcasted_iota(jnp.int32, shape, 1 - dim)).astype(jnp.bfloat16)

    def contract(left, right, dims):
        return lax.dot_general(
            left, right, ((dims[:1], dims[1:]), ((), ())), preferred_element_type=jnp.float32
        ).astype(jnp.bfloat16)

    upper = contract(
        contract(onehot((short, rank), 0), analysis_ref[...], (1, 0)),
        onehot((channels, long), 1),
        (1, 0),
    )
    keep = (
        lax.broadcasted_iota(jnp.int32, (short, long), 0) % rows
        == lax.broadcasted_iota(jnp.int32, (short, long), 1) % rows
    )
    wide_ref[...] = jnp.where(keep, upper.astype(jnp.float32), 0.0).astype(jnp.bfloat16)
    lower = contract(
        contract(onehot((long, channels), 0), basis_ref[...], (1, 1)),
        onehot((rank, short), 1),
        (1, 0),
    )
    keep = (
        lax.broadcasted_iota(jnp.int32, (long, short), 0) % rows
        == lax.broadcasted_iota(jnp.int32, (long, short), 1) % rows
    )
    tall_ref[...] = jnp.where(keep, lower.astype(jnp.float32), 0.0).astype(jnp.bfloat16)


def rows_kernel(count, wide_ref, tall_ref, band_ref, *refs):
    columns_refs, refs = refs[:count], refs[count:]
    sent_ref, bands_ref, held_ref, resampled_ref, done_ref, band_sems, in_sems, out_sems = refs
    parts, channels, part_rows, width = held_ref.shape
    rows = parts * part_rows
    size = channels // GROUPS

    def load(group):
        span = pl.ds(group * size, size)
        if count == 1:
            pairs = [(columns_refs[0].at[:, span], held_ref.at[:, span])]
        else:
            me = lax.axis_index("row")
            pairs = [
                (columns_refs[step].at[span], held_ref.at[partner(me, step, -1), span])
                for step in range(count)
            ]
        return [
            pltpu.make_async_copy(band_ref.at[span], bands_ref.at[span], band_sems.at[group])
        ] + [
            pltpu.make_async_copy(source, target, in_sems.at[group, step])
            for step, (source, target) in enumerate(pairs)
        ]

    for group in range(GROUPS):
        for copy in load(group):
            copy.start()

    def work(group, carry):
        for copy in load(group):
            copy.wait()
        for index in range(size):
            channel = group * size + index
            resampled_ref[channel] = jnp.dot(
                bands_ref[channel],
                held_ref[:, channel].reshape(rows, width),
                preferred_element_type=jnp.float32,
            ).astype(jnp.bfloat16)
        return carry

    lax.fori_loop(0, GROUPS, work, 0)
    owned = done_ref.shape[2]
    long = tall_ref.shape[0]
    steps = rows // (2 * part_rows)
    each = 2 * part_rows // owned

    def save(step):
        span = pl.ds(step * each, each)
        return pltpu.make_async_copy(done_ref.at[span], sent_ref.at[span], out_sems.at[step])

    for step in range(steps):
        start = step * 2 * part_rows
        block = jnp.concatenate(
            [
                resampled_ref[:, start : start + part_rows, :].reshape(long, width),
                resampled_ref[:, start + part_rows : start + 2 * part_rows, :].reshape(long, width),
            ],
            axis=1,
        )
        coefficients = jnp.dot(
            wide_ref[...], block, preferred_element_type=jnp.float32
        ).astype(jnp.bfloat16)
        model = jnp.dot(tall_ref[...], coefficients, preferred_element_type=jnp.float32)
        residual = block.astype(jnp.float32) - model
        for side in range(2):
            values = residual[:, side * width : (side + 1) * width].reshape(
                channels, part_rows // owned, owned, width
            )
            for part in range(part_rows // owned):
                done_ref[step * each + side * (part_rows // owned) + part] = values[
                    :, part
                ].astype(jnp.bfloat16)
        save(step).start()
    for step in range(steps):
        save(step).wait()


def combine_kernel(weights_ref, values_ref, *refs):
    map_ref = refs[-1]
    total, channels = values_ref.shape[0], values_ref.shape[1]
    for channel in range(channels):
        values = [values_ref[index, channel].astype(jnp.float32) for index in range(total)]
        sums = values
        while len(sums) > 1:
            sums = [left + right for left, right in zip(sums[::2], sums[1::2])]
        mean_level = sums[0] / total
        spread = jnp.zeros_like(mean_level)
        weighted = jnp.zeros_like(mean_level)
        for index in range(total):
            deviation = values[index] - mean_level
            spread = spread + deviation * deviation
            weighted = weighted + weights_ref[index] * deviation
        spread = spread / total + 1e-05
        map_ref[channel] = weighted / jnp.sqrt(total * spread)


def estimate(flops, moved):
    return pl.CostEstimate(flops=flops, bytes_accessed=moved, transcendentals=0)


def program(
    exposures,
    fake_flux,
    fake_rows,
    fake_cols,
    kernel_taps,
    band_offsets,
    analysis,
    spectral_basis,
    exposure_weights,
):
    _, channels, local_rows, width = exposures.shape
    row_parts = lax.axis_size("row")
    exp_parts = lax.axis_size("exp")
    rows = local_rows * row_parts
    owned = rows // exp_parts
    rank = analysis.shape[0]
    taps = kernel_taps.T
    flux = jnp.swapaxes(fake_flux, 1, 2)
    half_shape = (row_parts, channels, local_rows, LANES)
    out_shape = (exp_parts, channels, owned, LANES)
    bf16 = jnp.bfloat16
    dma = pltpu.SemaphoreType.DMA

    def resample_columns(half, count):
        shape = half_shape if count == 1 else half_shape[1:]
        return pl.pallas_call(
            functools.partial(columns_kernel, half, count),
            out_shape=[jax.ShapeDtypeStruct(shape, bf16)] * count,
            in_specs=[SMEM] * 5 + [ANY],
            out_specs=[ANY] * count,
            scratch_shapes=[
                pltpu.VMEM((channels, local_rows, width), bf16),
                pltpu.VMEM(half_shape, bf16),
                dma((GROUPS,)),
                dma((GROUPS, count)),
            ],
            cost_estimate=estimate(10**9, 4 * 10**6),
        )(fake_rows, fake_cols, band_offsets, taps, flux, exposures[0])

    def resample_rows(band, wide, tall, columns):
        count = len(columns)
        return pl.pallas_call(
            functools.partial(rows_kernel, count),
            out_shape=jax.ShapeDtypeStruct(out_shape, bf16),
            in_specs=[VMEM, VMEM, HBM] + [ANY] * count,
            out_specs=HBM,
            scratch_shapes=[
                pltpu.VMEM((channels, rows, rows), bf16),
                pltpu.VMEM(half_shape, bf16),
                pltpu.VMEM((channels, rows, LANES), bf16),
                pltpu.VMEM(out_shape, bf16),
                dma((GROUPS,)),
                dma((GROUPS, count)),
                dma((row_parts // 2,)),
            ],
            compiler_params=pltpu.CompilerParams(vmem_limit_bytes=GRANT),
            cost_estimate=estimate(10**9, 4 * 10**6),
        )(wide, tall, band, *columns)

    def combine(half, gathered, *started):
        size = channels // GROUPS
        return pl.pallas_call(
            combine_kernel,
            grid=(GROUPS,),
            out_shape=jax.ShapeDtypeStruct((channels, owned, 2 * LANES), jnp.float32),
            in_specs=[
                SMEM,
                pl.BlockSpec((exp_parts, size, owned, LANES), lambda step: (0, step, 0, 0)),
            ]
            + [ANY] * len(started),
            out_specs=pl.BlockSpec((size, owned, LANES), lambda step: (step, 0, half)),
            input_output_aliases={2: 0} if started else {},
            compiler_params=pltpu.CompilerParams(vmem_limit_bytes=GRANT),
            cost_estimate=estimate(10**7, 2 * 10**6),
        )(exposure_weights, gathered, *started)

    band, wide, tall = pl.pallas_call(
        prepare_kernel,
        out_shape=[
            jax.ShapeDtypeStruct((channels, rows, rows), bf16),
            jax.ShapeDtypeStruct((rank * local_rows, channels * local_rows), bf16),
            jax.ShapeDtypeStruct((channels * local_rows, rank * local_rows), bf16),
        ],
        in_specs=[SMEM, SMEM, VMEM, VMEM],
        out_specs=[VMEM] * 3,
        cost_estimate=estimate(10**7, 2 * 10**6),
        name="prepare",
    )(band_offsets, taps, analysis, spectral_basis.T)

    def exchange(value, axis):
        return lax.all_to_all(value, axis, split_axis=0, concat_axis=0, tiled=True)

    def shift(value, step):
        if step == 0:
            return value
        pairs = [(me, int(partner(me, step, 1))) for me in range(row_parts)]
        return lax.ppermute(value, "row", pairs)

    (first,) = resample_columns(0, 1)
    columns = [[exchange(first, "row")]]
    pieces = resample_columns(1, row_parts)
    columns.append([shift(value, step) for step, value in enumerate(pieces)])
    residual = [resample_rows(band, wide, tall, columns[half]) for half in range(2)]
    gathered = [exchange(value, "exp") for value in residual]
    return combine(1, gathered[1], combine(0, gathered[0]))


def solution(mesh):
    return jax.shard_map(
        program,
        mesh=mesh,
        in_specs=(
            P("exp", None, "row", None),
            P("exp", None, None),
            P(),
            P(),
            P(),
            P(),
            P(),
            P(),
            P(),
        ),
        out_specs=P(None, "exp", "row"),
        check_vma=False,
    )
```

time: 531 us -> 114 us (0.21)
  the two profiles are of different devices: /device:TPU:6 before, /device:TPU:1 now
where the time goes in v2:
time: 114 us
  waiting for transfers between devices  51.2 us (45%)
  Pallas kernels  31.2 us (27%)
  starting transfers between devices  26.2 us (23%)
  local copies, waits for them, and re-layouts  5.11 us (4%)
    all_to_all x3, waiting for transfers between devices, exchange(): return lax.all_to_all(value, axis, split_axis=0, concat_axis=0, tiled=True)  32.6 us
    all_to_all x3, starting transfers between devices, exchange(): return lax.all_to_all(value, axis, split_axis=0, concat_axis=0, tiled=True)  21.6 us
    ppermute x7, waiting for transfers between devices, shift(): return lax.ppermute(value, 'row', pairs)  18.6 us
    pallas_call x2, Pallas kernels, resample_columns(): pl.pallas_call(functools.partial(columns_kernel, half, count), out_shape=...  13.8 us
    pallas_call x2, Pallas kernels, resample_rows(): pl.pallas_call(functools.partial(rows_kernel, count), out_shape=jax.Shape...  9.72 us
    unnamed x18, local copies, waits for them, and re-layouts  5.11 us
    pallas_call x2, Pallas kernels, combine(): pl.pallas_call(combine_kernel, grid=(GROUPS,), out_shape=jax.ShapeDtypeSt...  4.76 us
    ppermute x7, starting transfers between devices, shift(): return lax.ppermute(value, 'row', pairs)  4.51 us
  transfers between devices with their start and end apart: 10, of which 5 were waited for; matrix products, arithmetic and copies ran while one was open for 0% of the time, Pallas kernels for 16%

profile of v2, /device:TPU:1, one launch (start us, length us, event | category | flops | bytes accessed | tf_op | source)
XLA Modules:
  0.0 113.8 jit_solution(12906619948028808212)
XLA Ops:
  0.0 6.7 %shard_map.93 = bf16[8,39,16,128]{3,2,1,0:T(8,128)(2,1)} custom-call(s32[16]{0:T(128)} %rows_ref.3, s32[16]{0:T(128)} %cols_ref.3, s32[39]{0:T(128)} %offsets_ref.5, f32[16,39]{1,0:T(8,128)} %bitcast.6, f32[1,16,39]{2,1,0:T(8,128)} %bitcast.9, bf16[39,16,2048]{2,1,0:T(8,128)(2,1)} %bitcast.4), custom_call_target="tpu_custom_call" | custom-call | flops 1000000000 | bytes 4000000 | tf_op jit(solution)/shard_map/pallas_call | solution.py:340
  6.8 6.7 %all-to-all-start.1 = ((bf16[8,39,16,128]{3,2,1,0:T(8,128)(2,1)}), bf16[8,39,16,128]{3,2,1,0:T(8,128)(2,1)S(1)}, u32[]{:S(2)}, u32[]{:S(2)}) async-start(bf16[8,39,16,128]{3,2,1,0:T(8,128)(2,1)} %shard_map.93), calls=%async_computation.1 | async-start | bytes 2555904 | tf_op jit(solution)/shard_map/all_to_all | solution.py:405
  13.5 2.9 %prepare.1 = (bf16[39,128,128]{2,1,0:T(8,128)(2,1)}, bf16[128,624]{1,0:T(8,128)(2,1)}, bf16[624,128]{1,0:T(8,128)(2,1)}) custom-call(s32[39]{0:T(128)} %offsets_ref.5, f32[16,39]{1,0:T(8,128)} %bitcast.7, bf16[8,39]{1,0:T(8,128)(2,1)} %analysis_ref.1, bf16[8,39]{1,0:T(8,128)(2,1)} %bitcast.11), custom_call_target="tpu_custom_call" | custom-call | flops 10000000 | bytes 2000000 | tf_op jit(solution)/shard_map/prepare/pallas_call | solution.py:391
  16.4 15.5 %all-to-all-done.1.refs_0_ = bf16[8,39,16,128]{3,2,1,0:T(8,128)(2,1)S(1)} async-done(((bf16[8,39,16,128]{3,2,1,0:T(8,128)(2,1)}), bf16[8,39,16,128]{3,2,1,0:T(8,128)(2,1)S(1)}, u32[]{:S(2)}, u32[]{:S(2)}) %all-to-all-start.1) | async-done | bytes 1277984 | tf_op jit(solution)/shard_map/all_to_all | solution.py:405
  31.8 0.0 copy-start
  31.8 1.3 %copy-done = bf16[39,128,128]{2,1,0:T(8,128)(2,1)S(1)} copy-done((bf16[39,128,128]{2,1,0:T(8,128)(2,1)S(1)}, bf16[39,128,128]{2,1,0:T(8,128)(2,1)}, u32[]{:S(2)}) %copy-start) | copy-done | bytes 1277976
  33.1 0.0 copy-start.3
  33.1 0.9 copy-done.3
  34.0 0.0 copy-start.5
  34.0 0.9 copy-done.5
  35.0 3.7 %shard_map.94 = bf16[16,39,8,128]{3,2,1,0:T(8,128)(2,1)} custom-call(bf16[128,624]{1,0:T(8,128)(2,1)S(1)} %copy-done.3, bf16[624,128]{1,0:T(8,128)(2,1)S(1)} %copy-done.5, bf16[39,128,128]{2,1,0:T(8,128)(2,1)S(1)} %copy-done, bf16[8,39,16,128]{3,2,1,0:T(8,128)(2,1)S(1)} %all-to-all-done.1.refs_0_), custom_call_target="tpu_custom_call" | custom-call | flops 1000000000 | bytes 4000000 | tf_op jit(solution)/shard_map/pallas_call | solution.py:356
  38.6 8.3 %all-to-all-start.2 = ((bf16[16,39,8,128]{3,2,1,0:T(8,128)(2,1)}), bf16[16,39,8,128]{3,2,1,0:T(8,128)(2,1)S(1)}, u32[]{:S(2)}, u32[]{:S(2)}) async-start(bf16[16,39,8,128]{3,2,1,0:T(8,128)(2,1)} %shard_map.94), calls=%async_computation.2 | async-start | bytes 2555904 | tf_op jit(solution)/shard_map/all_to_all | solution.py:405
  46.9 0.0 copy-start.1
  47.0 0.0 copy-start.4
  47.0 0.0 copy-start.6
  47.0 7.1 %shard_map.91 = (bf16[39,16,128]{2,1,0:T(8,128)(2,1)}, bf16[39,16,128]{2,1,0:T(8,128)(2,1)}, bf16[39,16,128]{2,1,0:T(8,128)(2,1)}, bf16[39,16,128]{2,1,0:T(8,128...) custom-call(s32[16]{0:T(128)} %rows_ref.3, ...), custom_call_target="tpu_custom_call" | custom-call | flops 1000000000 | bytes 4000000 | tf_op jit(solution)/shard_map/pallas_call | solution.py:340
  54.1 0.1 collective-permute-start
  54.1 1.4 %collective-permute-start.1 = (bf16[39,16,128]{2,1,0:T(8,128)(2,1)}, bf16[39,16,128]{2,1,0:T(8,128)(2,1)S(1)}, u32[]{:S(2)}, u32[]{:S(2)}) collective-permute-start(bf16[39,16,128]{2,1,0:T(8,128)(2,1)} %get-tuple-element.21), channel_id=1, source_target_pairs={{0,2},{1,3},{2,0},{3,1},{4,6},{5,7},{6,4},{7,5},{8,10},{9,11},{10,... | collective-permute-start | bytes 479240 | tf_op jit(solution)/shard_map/ppermute | solution.py:411
  55.5 2.0 %collective-permute-start.2 = (bf16[39,16,128]{2,1,0:T(8,128)(2,1)}, bf16[39,16,128]{2,1,0:T(8,128)(2,1)S(1)}, u32[]{:S(2)}, u32[]{:S(2)}) collective-permute-start(bf16[39,16,128]{2,1,0:T(8,128)(2,1)} %get-tuple-element.22), channel_id=1, source_target_pairs={{0,3},{1,0},{2,1},{3,2},{4,7},{5,4},{6,5},{7,6},{8,11},{9,8},{10,9... | collective-permute-start | bytes 479240 | tf_op jit(solution)/shard_map/ppermute | solution.py:411
  57.5 0.0 collective-permute-start.3
  57.5 1.1 collective-permute-start.4
  58.6 6.0 %collective-permute-done.refs_1_ = bf16[39,16,128]{2,1,0:T(8,128)(2,1)S(1)} collective-permute-done((bf16[39,16,128]{2,1,0:T(8,128)(2,1)}, bf16[39,16,128]{2,1,0:T(8,128)(2,1)S(1)}, u32[]{:S(2)}, u32[]{:S(2)}) %collective-permute-start) | collective-permute-done | bytes 159776 | tf_op jit(solution)/shard_map/ppermute | solution.py:411
  64.5 0.0 collective-permute-start.5
  64.5 0.0 collective-permute-done.1.refs_2_
  64.5 0.0 collective-permute-start.6
  64.6 0.3 collective-permute-done.2.refs_3_
  64.9 12.3 %collective-permute-done.3.refs_4_ = bf16[39,16,128]{2,1,0:T(8,128)(2,1)S(1)} collective-permute-done((bf16[39,16,128]{2,1,0:T(8,128)(2,1)}, bf16[39,16,128]{2,1,0:T(8,128)(2,1)S(1)}, u32[]{:S(2)}, u32[]{:S(2)}) %collective-permute-start.3) | collective-permute-done | bytes 159776 | tf_op jit(solution)/shard_map/ppermute | solution.py:411
  77.2 0.0 collective-permute-done.4.refs_5_
  77.2 0.0 collective-permute-done.5.refs_6_
  77.2 0.0 collective-permute-done.6.refs_7_
  77.2 0.0 copy-done.1
  77.2 0.0 copy-done.4
  77.2 0.0 copy-done.6
  77.2 0.0 copy-start.7
  77.2 0.9 copy-done.7
  78.2 6.0 %shard_map.92 = bf16[16,39,8,128]{3,2,1,0:T(8,128)(2,1)S(1)} custom-call(bf16[128,624]{1,0:T(8,128)(2,1)S(1)} %copy-done.4, bf16[624,128]{1,0:T(8,128)(2,1)S(1)} %copy-done.6, bf16[39,128,128]{2,1,0:T(8,128)(2,1)S(1)} %copy-done.1, bf16[39,16,128]{2,1,0:T(8,128)(2,1)S(1)} %copy-done.7, bf16[39,16,128]{2,1,0:T(8,128)(2,1)S(1)} %collective-permute-done.refs_1_, ...), custom_call_target="tpu_custom_call" | custom-call | flops 1000000000 | bytes 4000000 | tf_op jit(solution)/shard_map/pallas_call | solution.py:356
  84.2 0.0 copy-start.2
  84.2 1.0 copy-done.2
  85.3 0.0 copy-start.8
  85.3 0.0 all-to-all-done.2.values_ref
  85.3 6.6 %all-to-all-start = ((bf16[16,39,8,128]{3,2,1,0:T(8,128)(2,1)}), bf16[16,39,8,128]{3,2,1,0:T(8,128)(2,1)S(1)}, u32[]{:S(2)}, u32[]{:S(2)}) async-start(bf16[16,39,8,128]{3,2,1,0:T(8,128)(2,1)} %copy-done.2), calls=%async_computation | async-start | bytes 2555904 | tf_op jit(solution)/shard_map/all_to_all | solution.py:405
  91.9 0.0 copy-done.8
  91.9 2.4 %shard_map.95.refs_0_ = f32[39,8,256]{2,1,0:T(8,128)} custom-call(f32[16]{0:T(128)S(1)} %copy-done.8, bf16[16,39,8,128]{3,2,1,0:T(8,128)(2,1)S(1)} %all-to-all-done.2.values_ref), custom_call_target="tpu_custom_call" | custom-call | flops 10000000 | bytes 2000000 | tf_op jit(solution)/shard_map/pallas_call | solution.py:376
  94.3 17.1 %all-to-all-done.values_ref = bf16[16,39,8,128]{3,2,1,0:T(8,128)(2,1)S(1)} async-done(((bf16[16,39,8,128]{3,2,1,0:T(8,128)(2,1)}), bf16[16,39,8,128]{3,2,1,0:T(8,128)(2,1)S(1)}, u32[]{:S(2)}, u32[]{:S(2)}) %all-to-all-start) | async-done | bytes 1277984 | tf_op jit(solution)/shard_map/all_to_all | solution.py:405
  111.4 2.4 %shard_map.96 = f32[39,8,256]{2,1,0:T(8,128)} custom-call(f32[16]{0:T(128)S(1)} %copy-done.8, bf16[16,39,8,128]{3,2,1,0:T(8,128)(2,1)S(1)} %all-to-all-done.values_ref, f32[39,8,256]{2,1,0:T(8,128)} %shard_map.95.refs_0_), custom_call_target="tpu_custom_call", output_to_operand_aliasing={{}: (2, {})} | custom-call | flops 10000000 | bytes 2000000 | tf_op jit(solution)/shard_map/pallas_call | solution.py:376
Async XLA Ops:
  6.8 25.1 %all-to-all-start.1 = ((bf16[8,39,16,128]{3,2,1,0:T(8,128)(2,1)}), bf16[8,39,16,128]{3,2,1,0:T(8,128)(2,1)S(1)}, u32[]{:S(2)}, u32[]{:S(2)}) async-start(bf16[8,39,16,128]{3,2,1,0:T(8,128)(2,1)} %shard_map.93), calls=%async_computation.1 | async-start | bytes 2555904 | tf_op jit(solution)/shard_map/all_to_all | solution.py:405
  31.8 1.3 %copy-start = (bf16[39,128,128]{2,1,0:T(8,128)(2,1)S(1)}, bf16[39,128,128]{2,1,0:T(8,128)(2,1)}, u32[]{:S(2)}) copy-start(bf16[39,128,128]{2,1,0:T(8,128)(2,1)} %get-tuple-element.18.band_ref) | copy-start | bytes 3833860
  33.1 0.9 copy-start.3
  34.0 0.9 copy-start.5
  38.6 46.6 %all-to-all-start.2 = ((bf16[16,39,8,128]{3,2,1,0:T(8,128)(2,1)}), bf16[16,39,8,128]{3,2,1,0:T(8,128)(2,1)S(1)}, u32[]{:S(2)}, u32[]{:S(2)}) async-start(bf16[16,39,8,128]{3,2,1,0:T(8,128)(2,1)} %shard_map.94), calls=%async_computation.2 | async-start | bytes 2555904 | tf_op jit(solution)/shard_map/all_to_all | solution.py:405
  46.9 30.3 %copy-start.1 = (bf16[39,128,128]{2,1,0:T(8,128)(2,1)S(1)}, bf16[39,128,128]{2,1,0:T(8,128)(2,1)}, u32[]{:S(2)}) copy-start(bf16[39,128,128]{2,1,0:T(8,128)(2,1)} %get-tuple-element.18.band_ref) | copy-start | bytes 3833860
  47.0 30.3 %copy-start.4 = (bf16[128,624]{1,0:T(8,128)(2,1)S(1)}, bf16[128,624]{1,0:T(8,128)(2,1)}, u32[]{:S(2)}) copy-start(bf16[128,624]{1,0:T(8,128)(2,1)} %get-tuple-element.16.wide_ref) | copy-start | bytes 479236
  47.0 30.3 %copy-start.6 = (bf16[624,128]{1,0:T(8,128)(2,1)S(1)}, bf16[624,128]{1,0:T(8,128)(2,1)}, u32[]{:S(2)}) copy-start(bf16[624,128]{1,0:T(8,128)(2,1)} %get-tuple-element.17.tall_ref) | copy-start | bytes 479236
  54.1 10.5 %collective-permute-start = (bf16[39,16,128]{2,1,0:T(8,128)(2,1)}, bf16[39,16,128]{2,1,0:T(8,128)(2,1)S(1)}, u32[]{:S(2)}, u32[]{:S(2)}) collective-permute-start(bf16[39,16,128]{2,1,0:T(8,128)(2,1)} %get-tuple-element.20), channel_id=1, source_target_pairs={{0,1},{1,2},{2,3},{3,0},{4,5},{5,6},{6,7},{7,4},{8,9},{9,10},{10,1... | collective-permute-start | bytes 479240 | tf_op jit(solution)/shard_map/ppermute | solution.py:411
  54.1 10.4 %collective-permute-start.1 = (bf16[39,16,128]{2,1,0:T(8,128)(2,1)}, bf16[39,16,128]{2,1,0:T(8,128)(2,1)S(1)}, u32[]{:S(2)}, u32[]{:S(2)}) collective-permute-start(bf16[39,16,128]{2,1,0:T(8,128)(2,1)} %get-tuple-element.21), channel_id=1, source_target_pairs={{0,2},{1,3},{2,0},{3,1},{4,6},{5,7},{6,4},{7,5},{8,10},{9,11},{10,... | collective-permute-start | bytes 479240 | tf_op jit(solution)/shard_map/ppermute | solution.py:411
  55.5 9.3 %collective-permute-start.2 = (bf16[39,16,128]{2,1,0:T(8,128)(2,1)}, bf16[39,16,128]{2,1,0:T(8,128)(2,1)S(1)}, u32[]{:S(2)}, u32[]{:S(2)}) collective-permute-start(bf16[39,16,128]{2,1,0:T(8,128)(2,1)} %get-tuple-element.22), channel_id=1, source_target_pairs={{0,3},{1,0},{2,1},{3,2},{4,7},{5,4},{6,5},{7,6},{8,11},{9,8},{10,9... | collective-permute-start | bytes 479240 | tf_op jit(solution)/shard_map/ppermute | solution.py:411
  57.5 19.7 %collective-permute-start.3 = (bf16[39,16,128]{2,1,0:T(8,128)(2,1)}, bf16[39,16,128]{2,1,0:T(8,128)(2,1)S(1)}, u32[]{:S(2)}, u32[]{:S(2)}) collective-permute-start(bf16[39,16,128]{2,1,0:T(8,128)(2,1)} %get-tuple-element.23), channel_id=1, source_target_pairs={{0,4},{1,5},{2,6},{3,7},{4,0},{5,1},{6,2},{7,3},{8,12},{9,13},{10,... | collective-permute-start | bytes 479240 | tf_op jit(solution)/shard_map/ppermute | solution.py:411
  57.5 19.7 %collective-permute-start.4 = (bf16[39,16,128]{2,1,0:T(8,128)(2,1)}, bf16[39,16,128]{2,1,0:T(8,128)(2,1)S(1)}, u32[]{:S(2)}, u32[]{:S(2)}) collective-permute-start(bf16[39,16,128]{2,1,0:T(8,128)(2,1)} %get-tuple-element.24), channel_id=1, source_target_pairs={{0,5},{1,6},{2,7},{3,4},{4,1},{5,2},{6,3},{7,0},{8,13},{9,14},{10,... | collective-permute-start | bytes 479240 | tf_op jit(solution)/shard_map/ppermute | solution.py:411
  64.5 12.7 %collective-permute-start.5 = (bf16[39,16,128]{2,1,0:T(8,128)(2,1)}, bf16[39,16,128]{2,1,0:T(8,128)(2,1)S(1)}, u32[]{:S(2)}, u32[]{:S(2)}) collective-permute-start(bf16[39,16,128]{2,1,0:T(8,128)(2,1)} %get-tuple-element.25), channel_id=1, source_target_pairs={{0,6},{1,7},{2,4},{3,5},{4,2},{5,3},{6,0},{7,1},{8,14},{9,15},{10,... | collective-permute-start | bytes 479240 | tf_op jit(solution)/shard_map/ppermute | solution.py:411
  64.5 12.7 %collective-permute-start.6 = (bf16[39,16,128]{2,1,0:T(8,128)(2,1)}, bf16[39,16,128]{2,1,0:T(8,128)(2,1)S(1)}, u32[]{:S(2)}, u32[]{:S(2)}) collective-permute-start(bf16[39,16,128]{2,1,0:T(8,128)(2,1)} %get-tuple-element.26), channel_id=1, source_target_pairs={{0,7},{1,4},{2,5},{3,6},{4,3},{5,0},{6,1},{7,2},{8,15},{9,12},{10,... | collective-permute-start | bytes 479240 | tf_op jit(solution)/shard_map/ppermute | solution.py:411
  77.2 0.9 copy-start.7
  84.2 1.1 copy-start.2
  85.3 6.6 %copy-start.8 = (f32[16]{0:T(128)S(1)}, f32[16]{0:T(128)}, u32[]{:S(2)}) copy-start(f32[16]{0:T(128)} %weights_ref.3) | copy-start | bytes 196
  85.3 26.1 %all-to-all-start = ((bf16[16,39,8,128]{3,2,1,0:T(8,128)(2,1)}), bf16[16,39,8,128]{3,2,1,0:T(8,128)(2,1)S(1)}, u32[]{:S(2)}, u32[]{:S(2)}) async-start(bf16[16,39,8,128]{3,2,1,0:T(8,128)(2,1)} %copy-done.2), calls=%async_computation | async-start | bytes 2555904 | tf_op jit(solution)/shard_map/all_to_all | solution.py:405

commit v3 on v2

v3 whole, which is shorter than its diff:
```python
import functools

import jax
import jax.numpy as jnp
from jax import lax
from jax.experimental import pallas as pl
from jax.experimental.pallas import tpu as pltpu
from jax.sharding import PartitionSpec as P


LANES = 128
NEAR = 64
GROUPS = 3
RING = 4
GRANT = 20 * 2**20
VMEM = pl.BlockSpec(memory_space=pltpu.VMEM)
SMEM = pl.BlockSpec(memory_space=pltpu.SMEM)
ANY = pl.BlockSpec(memory_space=pl.ANY)
HBM = pl.BlockSpec(memory_space=pltpu.HBM)


def circulant(taps_ref, offsets_ref, channel, sign):
    lane = lax.broadcasted_iota(jnp.int32, (8, LANES), 1)
    signed = jnp.where(lane < NEAR, lane, lane - LANES)
    place = sign * signed - offsets_ref[channel]
    values = jnp.zeros((8, LANES), jnp.float32)
    for tap_index in range(taps_ref.shape[0]):
        values = jnp.where(place == tap_index, taps_ref[tap_index, channel], values)
    rows = jnp.concatenate([values] * (LANES // 8), axis=0)
    return pltpu.roll(rows, 0, 1, stride=1, stride_axis=0)


def partner(me, step, sign):
    return (me // RING ^ step // RING) * RING + (me + sign * step) % RING


def chip_partner(chip, step, sign):
    return (chip // 2 + sign * (step // 2)) % RING * 2 + (chip % 2 ^ step % 2)


def gaps():
    inner = lax.broadcasted_iota(jnp.int32, (LANES, LANES), 0)
    outer = lax.broadcasted_iota(jnp.int32, (LANES, LANES), 1)
    return jnp.abs(outer - inner)


def find_local(rows_ref, cols_ref, list_ref, kind_ref, local_rows):
    row_start = lax.axis_index("row") * local_rows

    def look(which, found):
        local = rows_ref[which] - row_start
        list_ref[found] = which
        return found + jnp.where((local >= 0) & (local < local_rows), 1, 0)

    found = lax.fori_loop(0, rows_ref.shape[0], look, jnp.int32(0))

    def sort(place, carry):
        row, column = rows_ref[list_ref[place]], cols_ref[list_ref[place]]

        def compare(other, counts):
            which = list_ref[other]
            same = (rows_ref[which] == row) & (cols_ref[which] == column)
            return (
                counts[0] + jnp.where(same & (other < place), 1, 0),
                counts[1] + jnp.where(same & (other > place), 1, 0),
            )

        earlier, later = lax.fori_loop(0, found, compare, (jnp.int32(0), jnp.int32(0)))
        kind_ref[place] = jnp.where(earlier > 0, 0, jnp.where(later > 0, 2, 1))
        return carry

    lax.fori_loop(0, found, sort, 0)
    return found


def inject(
    found, list_ref, kind_ref, rows_ref, cols_ref, flux_ref, held_ref, first_channel, channels
):
    local_rows = held_ref.shape[1]
    row_start = lax.axis_index("row") * local_rows

    def one(place, carry):
        which, kind = list_ref[place], kind_ref[place]
        row, column = rows_ref[which], cols_ref[which]
        start = pl.multiple_of((column // LANES) * LANES, LANES)
        row_ids = lax.broadcasted_iota(jnp.int32, (local_rows, LANES), 0)
        col_ids = lax.broadcasted_iota(jnp.int32, (local_rows, LANES), 1)
        hit = (row_ids == row - row_start) & (col_ids == column - start)

        def add(channel, total):
            tile = held_ref[channel, :, pl.ds(start, LANES)].astype(jnp.float32)
            held_ref[channel, :, pl.ds(start, LANES)] = jnp.where(
                hit, tile + total, tile
            ).astype(jnp.bfloat16)

        @pl.when(kind == 1)
        def _():
            for index in range(channels):
                channel = first_channel + index
                add(channel, flux_ref[0, which, channel])

        @pl.when(kind == 2)
        def _():
            def shared(index, inner):
                channel = first_channel + index

                def gather(other, total):
                    same = (rows_ref[other] == row) & (cols_ref[other] == column)
                    return total + jnp.where(same, flux_ref[0, other, channel], 0.0)

                add(channel, lax.fori_loop(0, rows_ref.shape[0], gather, jnp.float32(0.0)))
                return inner

            lax.fori_loop(0, channels, shared, 0)

        return carry

    lax.fori_loop(0, found, one, 0)


def columns_kernel(half, count, rows_ref, cols_ref, flux_ref, frames_ref, *refs):
    if half == 0:
        (offsets_ref, taps_ref), refs = refs[:2], refs[2:]
        ring_in_ref = None
    else:
        ring_in_ref, refs = refs[0], refs[1:]
    sent_refs, refs = refs[:count], refs[count:]
    if half == 0:
        ring_out_ref, refs = refs[0], refs[1:]
    held_ref, done_ref, ring_ref, list_ref, kind_ref, in_sems, out_sems, ring_sems = refs
    channels, local_rows, width = held_ref.shape
    size = channels // GROUPS
    blocks = width // LANES

    def loads(group):
        span = pl.ds(group * size, size)
        copies = [
            pltpu.make_async_copy(frames_ref.at[span], held_ref.at[span], in_sems.at[group])
        ]
        if half == 1:
            copies.append(
                pltpu.make_async_copy(
                    ring_in_ref.at[span], ring_ref.at[span], ring_sems.at[group]
                )
            )
        return copies

    def saves(group):
        span = pl.ds(group * size, size)
        if count == 1:
            pairs = [(done_ref.at[:, span], sent_refs[0].at[:, span])]
        else:
            me = lax.axis_index("row")
            pairs = [
                (done_ref.at[partner(me, step, 1), span], sent_refs[step].at[span])
                for step in range(count)
            ]
        copies = [
            pltpu.make_async_copy(source, target, out_sems.at[group, step])
            for step, (source, target) in enumerate(pairs)
        ]
        if half == 0:
            copies.append(
                pltpu.make_async_copy(
                    ring_ref.at[span], ring_out_ref.at[span], ring_sems.at[group]
                )
            )
        return copies

    for group in range(GROUPS):
        for copy in loads(group):
            copy.start()
    found = find_local(rows_ref, cols_ref, list_ref, kind_ref, local_rows)
    gap = gaps()
    lane = lax.broadcasted_iota(jnp.int32, (local_rows, LANES), 1)
    edge = jnp.zeros((local_rows, LANES), jnp.bfloat16)

    def work(group, carry):
        for copy in loads(group):
            copy.wait()
        inject(
            found,
            list_ref,
            kind_ref,
            rows_ref,
            cols_ref,
            flux_ref,
            held_ref,
            group * size,
            size,
        )
        for index in range(size):
            channel = group * size + index
            if half == 0:
                ring = circulant(taps_ref, offsets_ref, channel, -1).astype(jnp.bfloat16)
                ring_ref[channel] = ring
            else:
                ring = ring_ref[channel]
            weights = jnp.concatenate(
                [
                    jnp.where(gap < NEAR, ring, jnp.zeros_like(ring)),
                    jnp.where(gap >= NEAR, ring, jnp.zeros_like(ring)),
                ],
                axis=0,
            )
            lines = []
            for block in range(half, blocks, 2):
                start = block * LANES
                here = held_ref[channel, :, start : start + LANES]
                after = held_ref[channel, :, start + LANES : start + 2 * LANES] if block < blocks - 1 else edge
                before = held_ref[channel, :, start - LANES : start] if block > 0 else edge
                lines.append(
                    jnp.concatenate([here, jnp.where(lane < NEAR, after, before)], axis=1)
                )
            result = jnp.dot(
                jnp.concatenate(lines, axis=0), weights, preferred_element_type=jnp.float32
            ).astype(jnp.bfloat16)
            for piece in range(blocks // 2):
                done_ref[piece, channel] = result[piece * local_rows : (piece + 1) * local_rows]
        for copy in saves(group):
            copy.start()
        return carry

    lax.fori_loop(0, GROUPS, work, 0)
    for group in range(GROUPS):
        for copy in saves(group):
            copy.wait()


def prepare_kernel(offsets_ref, taps_ref, analysis_ref, basis_ref, band_ref, wide_ref, tall_ref):
    channels = band_ref.shape[0]
    size = channels // GROUPS
    gap = gaps()

    def work(group, carry):
        for index in range(size):
            channel = group * size + index
            ring = circulant(taps_ref, offsets_ref, channel, 1)
            band_ref[channel] = jnp.where(gap < NEAR, ring, 0.0).astype(jnp.bfloat16)
        return carry

    lax.fori_loop(0, GROUPS, work, 0)
    rank = analysis_ref.shape[0]
    short, long = wide_ref.shape
    rows = short // rank

    def onehot(shape, dim):
        left = lax.broadcasted_iota(jnp.int32, shape, dim) // rows
        return (left == lax.broadcasted_iota(jnp.int32, shape, 1 - dim)).astype(jnp.bfloat16)

    def contract(left, right, dims):
        return lax.dot_general(
            left, right, ((dims[:1], dims[1:]), ((), ())), preferred_element_type=jnp.float32
        ).astype(jnp.bfloat16)

    upper = contract(
        contract(onehot((short, rank), 0), analysis_ref[...], (1, 0)),
        onehot((channels, long), 1),
        (1, 0),
    )
    keep = (
        lax.broadcasted_iota(jnp.int32, (short, long), 0) % rows
        == lax.broadcasted_iota(jnp.int32, (short, long), 1) % rows
    )
    wide_ref[...] = jnp.where(keep, upper.astype(jnp.float32), 0.0).astype(jnp.bfloat16)
    lower = contract(
        contract(onehot((long, channels), 0), basis_ref[...], (1, 1)),
        onehot((rank, short), 1),
        (1, 0),
    )
    keep = (
        lax.broadcasted_iota(jnp.int32, (long, short), 0) % rows
        == lax.broadcasted_iota(jnp.int32, (long, short), 1) % rows
    )
    tall_ref[...] = jnp.where(keep, lower.astype(jnp.float32), 0.0).astype(jnp.bfloat16)


def rows_kernel(count, chips, wide_ref, tall_ref, band_ref, *refs):
    columns_refs, refs = refs[:count], refs[count:]
    sent_refs, refs = refs[:chips], refs[chips:]
    held_ref, resampled_ref, done_ref, out_sems = refs
    parts, channels, part_rows, width = resampled_ref.shape
    size = channels // GROUPS
    if count > 1:
        me = lax.axis_index("row")
        for step in range(count):
            held_ref[partner(me, step, -1)] = columns_refs[step][...]
        values_ref = held_ref
    else:
        values_ref = columns_refs[0]

    def work(group, carry):
        for index in range(size):
            channel = group * size + index
            result = jnp.dot(
                band_ref[channel],
                values_ref[:, channel].reshape(parts * part_rows, width),
                preferred_element_type=jnp.float32,
            ).astype(jnp.bfloat16)
            for part in range(parts):
                resampled_ref[part, channel] = result[part * part_rows : (part + 1) * part_rows]
        return carry

    lax.fori_loop(0, GROUPS, work, 0)
    owned = done_ref.shape[2]
    long = tall_ref.shape[0]
    steps = parts // 2
    each = 2 * part_rows // owned
    mine = lax.axis_index("exp") // 2

    def save(step):
        span = pl.ds(step * each, each)
        return pltpu.make_async_copy(done_ref.at[span], sent_refs[0].at[span], out_sems.at[step])

    for step in range(steps):
        if chips == 1:
            places = [2 * step, 2 * step + 1]
        else:
            places = [chip_partner(mine, 2 * step + side, 1) for side in range(2)]
        block = jnp.concatenate(
            [resampled_ref[place].reshape(long, width) for place in places], axis=1
        )
        coefficients = jnp.dot(
            wide_ref[...], block, preferred_element_type=jnp.float32
        ).astype(jnp.bfloat16)
        model = jnp.dot(tall_ref[...], coefficients, preferred_element_type=jnp.float32)
        residual = block.astype(jnp.float32) - model
        for side in range(2):
            values = residual[:, side * width : (side + 1) * width].reshape(
                channels, part_rows // owned, owned, width
            )
            for part in range(part_rows // owned):
                piece = values[:, part].astype(jnp.bfloat16)
                if chips == 1:
                    done_ref[step * each + side * (part_rows // owned) + part] = piece
                else:
                    sent_refs[2 * step + side][part] = piece
        if chips == 1:
            save(step).start()
    if chips == 1:
        for step in range(steps):
            save(step).wait()


def forward_kernel(*refs):
    given, kept_ref = refs[:-1], refs[-1]
    other = 1 - lax.axis_index("exp") % 2
    for index, ref in enumerate(given):
        kept_ref[index] = ref[other]


def combine_channel(sources, channel):
    total = len(sources)
    values = [ref[index, channel].astype(jnp.float32) for ref, index, _ in sources]
    sums = values
    while len(sums) > 1:
        sums = [left + right for left, right in zip(sums[::2], sums[1::2])]
    mean_level = sums[0] / total
    spread = jnp.zeros_like(mean_level)
    weighted = jnp.zeros_like(mean_level)
    for value, (_, _, weight) in zip(values, sources):
        deviation = value - mean_level
        spread = spread + deviation * deviation
        weighted = weighted + weight * deviation
    spread = spread / total + 1e-05
    return weighted / jnp.sqrt(total * spread)


def combine_kernel(weights_ref, values_ref, map_ref):
    channels = map_ref.shape[0]
    size = channels // GROUPS
    sources = [
        (values_ref, index, weights_ref[index]) for index in range(values_ref.shape[0])
    ]

    def work(group, carry):
        for index in range(size):
            map_ref[group * size + index] = combine_channel(sources, group * size + index)
        return carry

    lax.fori_loop(0, GROUPS, work, 0)


def finish_kernel(weights_ref, first_ref, swapped_ref, *refs):
    kept_refs, (map_ref, held_ref, sems) = refs[:-3], refs[-3:]
    channels = held_ref.shape[0]
    size = channels // GROUPS
    me = lax.axis_index("exp")
    core = me % 2
    sources = []
    for step, ref in enumerate(kept_refs):
        chip = chip_partner(me // 2, step, -1)
        sources.append((ref, core, weights_ref[2 * chip + core]))
        sources.append((swapped_ref, step, weights_ref[2 * chip + 1 - core]))

    def save(group):
        span = pl.ds(group * size, size)
        return pltpu.make_async_copy(held_ref.at[span], map_ref.at[span], sems.at[group])

    def work(group, carry):
        for index in range(size):
            channel = group * size + index
            held_ref[channel, :, :LANES] = first_ref[channel]
            held_ref[channel, :, LANES:] = combine_channel(sources, channel)
        save(group).start()
        return carry

    lax.fori_loop(0, GROUPS, work, 0)
    for group in range(GROUPS):
        save(group).wait()


def estimate(flops, moved):
    return pl.CostEstimate(flops=flops, bytes_accessed=moved, transcendentals=0)


def program(
    exposures,
    fake_flux,
    fake_rows,
    fake_cols,
    kernel_taps,
    band_offsets,
    analysis,
    spectral_basis,
    exposure_weights,
):
    _, channels, local_rows, width = exposures.shape
    row_parts = lax.axis_size("row")
    exp_parts = lax.axis_size("exp")
    rows = local_rows * row_parts
    owned = rows // exp_parts
    rank = analysis.shape[0]
    taps = kernel_taps.T
    flux = jnp.swapaxes(fake_flux, 1, 2)
    half_shape = (row_parts, channels, local_rows, LANES)
    out_shape = (exp_parts, channels, owned, LANES)
    bf16 = jnp.bfloat16
    dma = pltpu.SemaphoreType.DMA

    def resample_columns(half, count, *weights):
        shape = half_shape if count == 1 else half_shape[1:]
        square = (channels, LANES, LANES)
        rings = 1 if half == 0 else 0
        return pl.pallas_call(
            functools.partial(columns_kernel, half, count),
            out_shape=[jax.ShapeDtypeStruct(shape, bf16)] * count
            + [jax.ShapeDtypeStruct(square, bf16)] * rings,
            in_specs=[SMEM] * 3 + [ANY] + ([SMEM] * 2 if half == 0 else [ANY]),
            out_specs=[ANY] * (count + rings),
            scratch_shapes=[
                pltpu.VMEM((channels, local_rows, width), bf16),
                pltpu.VMEM(half_shape, bf16),
                pltpu.VMEM(square, bf16),
                pltpu.SMEM((fake_rows.shape[0] + 1,), jnp.int32),
                pltpu.SMEM((fake_rows.shape[0] + 1,), jnp.int32),
                dma((GROUPS,)),
                dma((GROUPS, count)),
                dma((GROUPS,)),
            ],
            cost_estimate=estimate(10**9, 4 * 10**6),
        )(fake_rows, fake_cols, flux, exposures[0], *weights)

    def resample_rows(chips, band, wide, tall, columns):
        count = len(columns)
        shape = (exp_parts // chips,) + out_shape[1:]
        return pl.pallas_call(
            functools.partial(rows_kernel, count, chips),
            out_shape=[jax.ShapeDtypeStruct(shape, bf16)] * chips,
            in_specs=[VMEM] * (3 + count),
            out_specs=[ANY if chips == 1 else VMEM] * chips,
            scratch_shapes=[
                pltpu.VMEM(half_shape, bf16),
                pltpu.VMEM(half_shape, bf16),
                pltpu.VMEM(out_shape, bf16),
                dma((row_parts // 2,)),
            ],
            compiler_params=pltpu.CompilerParams(vmem_limit_bytes=GRANT),
            cost_estimate=estimate(10**9, 4 * 10**6),
        )(wide, tall, band, *columns)

    def forward(given):
        return pl.pallas_call(
            forward_kernel,
            out_shape=jax.ShapeDtypeStruct((len(given),) + out_shape[1:], bf16),
            in_specs=[VMEM] * len(given),
            out_specs=VMEM,
            compiler_params=pltpu.CompilerParams(vmem_limit_bytes=GRANT),
            cost_estimate=estimate(0, 2 * 10**6),
            name="forward",
        )(*given)

    def combine(gathered):
        return pl.pallas_call(
            combine_kernel,
            out_shape=jax.ShapeDtypeStruct(out_shape[1:], jnp.float32),
            in_specs=[SMEM, VMEM],
            out_specs=VMEM,
            compiler_params=pltpu.CompilerParams(vmem_limit_bytes=GRANT),
            cost_estimate=estimate(10**7, 2 * 10**6),
            name="combine",
        )(exposure_weights, gathered)

    def finish(first, swapped, kept):
        shape = (channels, owned, 2 * LANES)
        return pl.pallas_call(
            finish_kernel,
            out_shape=jax.ShapeDtypeStruct(shape, jnp.float32),
            in_specs=[SMEM] + [VMEM] * (2 + len(kept)),
            out_specs=ANY,
            scratch_shapes=[pltpu.VMEM(shape, jnp.float32), dma((GROUPS,))],
            compiler_params=pltpu.CompilerParams(vmem_limit_bytes=GRANT),
            cost_estimate=estimate(10**7, 2 * 10**6),
            name="finish",
        )(exposure_weights, first, swapped, *kept)

    band, wide, tall = pl.pallas_call(
        prepare_kernel,
        out_shape=[
            jax.ShapeDtypeStruct((channels, rows, rows), bf16),
            jax.ShapeDtypeStruct((rank * local_rows, channels * local_rows), bf16),
            jax.ShapeDtypeStruct((channels * local_rows, rank * local_rows), bf16),
        ],
        in_specs=[SMEM, SMEM, VMEM, VMEM],
        out_specs=[VMEM] * 3,
        compiler_params=pltpu.CompilerParams(vmem_limit_bytes=GRANT),
        cost_estimate=estimate(10**7, 2 * 10**6),
        name="prepare",
    )(band_offsets, taps, analysis, spectral_basis.T)

    def exchange(value, axis):
        return lax.all_to_all(value, axis, split_axis=0, concat_axis=0, tiled=True)

    def shift(value, step):
        if step == 0:
            return value
        pairs = [(me, int(partner(me, step, 1))) for me in range(row_parts)]
        return lax.ppermute(value, "row", pairs)

    first, ring = resample_columns(0, 1, band_offsets, taps)
    columns = [[exchange(first, "row")]]
    pieces = resample_columns(1, row_parts, ring)
    columns.append([shift(value, step) for step, value in enumerate(pieces)])
    (residual,) = resample_rows(1, band, wide, tall, columns[0])
    gathered = exchange(residual, "exp")
    pieces = resample_rows(exp_parts // 2, band, wide, tall, columns[1])

    def pass_on(value, step):
        if step == 0:
            return value
        pairs = [
            (me, int(chip_partner(me // 2, step, 1)) * 2 + me % 2) for me in range(exp_parts)
        ]
        return lax.ppermute(value, "exp", pairs)

    kept = [pass_on(value, step) for step, value in enumerate(pieces)]
    swapped = lax.ppermute(forward(kept), "exp", [(me, me ^ 1) for me in range(exp_parts)])
    return finish(combine(gathered), swapped, kept)


def solution(mesh):
    return jax.shard_map(
        program,
        mesh=mesh,
        in_specs=(
            P("exp", None, "row", None),
            P("exp", None, None),
            P(),
            P(),
            P(),
            P(),
            P(),
            P(),
            P(),
        ),
        out_specs=P(None, "exp", "row"),
        check_vma=False,
    )
```

time: 114 us -> 91 us (0.80)
  the two profiles are of different devices: /device:TPU:1 before, /device:TPU:3 now
where the time goes in v3:
time: 91 us; the launch traced here: 90.6 us
  starting transfers between devices  43.8 us (48%)
  waiting for transfers between devices  22.8 us (25%)
  Pallas kernels  20.9 us (23%)
  local copies, waits for them, and re-layouts  2.93 us (3%)
    all_to_all x2, starting transfers between devices, exchange(): return lax.all_to_all(value, axis, split_axis=0, concat_axis=0, tiled=True)  16.8 us
    ppermute x7, waiting for transfers between devices, pass_on(): return lax.ppermute(value, 'exp', pairs)  16 us
    ppermute x7, starting transfers between devices, pass_on(): return lax.ppermute(value, 'exp', pairs)  14.2 us
    ppermute x7, starting transfers between devices, shift(): return lax.ppermute(value, 'row', pairs)  11.5 us
    pallas_call x2, Pallas kernels, resample_columns(): pl.pallas_call(functools.partial(columns_kernel, half, count), out_shape=...  9.18 us
    ppermute x7, waiting for transfers between devices, shift(): return lax.ppermute(value, 'row', pairs)  6.5 us
    pallas_call x2, Pallas kernels, resample_rows(): pl.pallas_call(functools.partial(rows_kernel, count, chips), out_shape=[j...  6.16 us
    unnamed x24, local copies, waits for them, and re-layouts  2.93 us
  transfers between devices with their start and end apart: 17, of which 6 were waited for; matrix products, arithmetic and copies ran while one was open for 0% of the time, Pallas kernels for 16%

profile of v3, /device:TPU:3, one launch (start us, length us, event | category | flops | bytes accessed | tf_op | source)
XLA Modules:
  0.0 90.6 jit_solution(2163963842977370168)
XLA Ops:
  0.0 4.6 %shard_map.91 = (bf16[8,39,16,128]{3,2,1,0:T(8,128)(2,1)}, bf16[39,128,128]{2,1,0:T(8,128)(2,1)}) custom-call(s32[16]{0:T(128)} %rows_ref.3, s32[16]{0:T(128)} %cols_ref.3, f32[1,16,39]{2,1,0:T(8,128)} %bitcast.9, bf16[39,16,2048]{2,1,0:T(8,128)(2,1)} %bitcast.7, s32[39]{0:T(128)} %refs_0_.1, f32[16,39]{1,0:T(8,128)} %bitcast.4), custom_call_target="tpu_custom_call" | custom-call | flops 1000000000 | bytes 4000000 | tf_op jit(solution)/shard_map/pallas_call | solution.py:445
  4.6 5.8 %all-to-all-start = ((bf16[8,39,16,128]{3,2,1,0:T(8,128)(2,1)}), bf16[8,39,16,128]{3,2,1,0:T(8,128)(2,1)S(1)}, u32[]{:S(2)}, u32[]{:S(2)}) async-start(bf16[8,39,16,128]{3,2,1,0:T(8,128)(2,1)} %get-tuple-element.29), calls=%async_computation | async-start | bytes 2555904 | tf_op jit(solution)/shard_map/all_to_all | solution.py:532
  10.5 0.0 copy-start.11
  10.5 4.6 %shard_map.93 = (bf16[39,16,128]{2,1,0:T(8,128)(2,1)}, bf16[39,16,128]{2,1,0:T(8,128)(2,1)}, bf16[39,16,128]{2,1,0:T(8,128)(2,1)}, bf16[39,16,128]{2,1,0:T(8,128...) custom-call(s32[16]{0:T(128)} %rows_ref.3, ...), custom_call_target="tpu_custom_call" | custom-call | flops 1000000000 | bytes 4000000 | tf_op jit(solution)/shard_map/pallas_call | solution.py:445
  15.1 1.8 %collective-permute-start = (bf16[39,16,128]{2,1,0:T(8,128)(2,1)}, bf16[39,16,128]{2,1,0:T(8,128)(2,1)S(1)}, u32[]{:S(2)}, u32[]{:S(2)}) collective-permute-start(bf16[39,16,128]{2,1,0:T(8,128)(2,1)} %get-tuple-element.32), channel_id=1, source_target_pairs={{0,1},{1,2},{2,3},{3,0},{4,5},{5,6},{6,7},{7,4},{8,9},{9,10},{10,1... | collective-permute-start | bytes 479240 | tf_op jit(solution)/shard_map/ppermute | solution.py:538
  16.8 0.5 collective-permute-start.1
  17.3 1.9 %collective-permute-start.2 = (bf16[39,16,128]{2,1,0:T(8,128)(2,1)}, bf16[39,16,128]{2,1,0:T(8,128)(2,1)S(1)}, u32[]{:S(2)}, u32[]{:S(2)}) collective-permute-start(bf16[39,16,128]{2,1,0:T(8,128)(2,1)} %get-tuple-element.34), channel_id=1, source_target_pairs={{0,3},{1,0},{2,1},{3,2},{4,7},{5,4},{6,5},{7,6},{8,11},{9,8},{10,9... | collective-permute-start | bytes 479240 | tf_op jit(solution)/shard_map/ppermute | solution.py:538
  19.2 1.5 %collective-permute-start.3 = (bf16[39,16,128]{2,1,0:T(8,128)(2,1)}, bf16[39,16,128]{2,1,0:T(8,128)(2,1)}, u32[]{:S(2)}, u32[]{:S(2)}) collective-permute-start(bf16[39,16,128]{2,1,0:T(8,128)(2,1)} %get-tuple-element.35), channel_id=1, source_target_pairs={{0,4},{1,5},{2,6},{3,7},{4,0},{5,1},{6,2},{7,3},{8,12},{9,13},{10,... | collective-permute-start | bytes 479240 | tf_op jit(solution)/shard_map/ppermute | solution.py:538
  20.7 0.0 collective-permute-start.4
  20.7 2.1 %prepare.1 = (bf16[39,128,128]{2,1,0:T(8,128)(2,1)S(1)}, bf16[128,624]{1,0:T(8,128)(2,1)S(1)}, bf16[624,128]{1,0:T(8,128)(2,1)S(1)}) custom-call(s32[39]{0:T(128)S(1)} %copy-done.11, f32[16,39]{1,0:T(8,128)S(1)} %bitcast.5, bf16[8,39]{1,0:T(8,128)(2,1)S(1)} %copy-done.9, bf16[8,39]{1,0:T(8,128)(2,1)S(1)} %bitcast.6), custom_call_target="tpu_custom_call" | custom-call | flops 10000000 | bytes 2000000 | tf_op jit(solution)/shard_map/prepare/pallas_call | solution.py:517
  22.8 6.5 %collective-permute-done.refs_1_ = bf16[39,16,128]{2,1,0:T(8,128)(2,1)S(1)} collective-permute-done((bf16[39,16,128]{2,1,0:T(8,128)(2,1)}, bf16[39,16,128]{2,1,0:T(8,128)(2,1)S(1)}, u32[]{:S(2)}, u32[]{:S(2)}) %collective-permute-start) | collective-permute-done | bytes 159776 | tf_op jit(solution)/shard_map/ppermute | solution.py:538
  29.3 1.8 %collective-permute-start.5 = (bf16[39,16,128]{2,1,0:T(8,128)(2,1)}, bf16[39,16,128]{2,1,0:T(8,128)(2,1)}, u32[]{:S(2)}, u32[]{:S(2)}) collective-permute-start(bf16[39,16,128]{2,1,0:T(8,128)(2,1)} %get-tuple-element.37), channel_id=1, source_target_pairs={{0,6},{1,7},{2,4},{3,5},{4,2},{5,3},{6,0},{7,1},{8,14},{9,15},{10,... | collective-permute-start | bytes 479240 | tf_op jit(solution)/shard_map/ppermute | solution.py:538
  31.1 0.0 collective-permute-done.1.refs_2_
  31.1 4.0 %collective-permute-start.6 = (bf16[39,16,128]{2,1,0:T(8,128)(2,1)}, bf16[39,16,128]{2,1,0:T(8,128)(2,1)}, u32[]{:S(2)}, u32[]{:S(2)}) collective-permute-start(bf16[39,16,128]{2,1,0:T(8,128)(2,1)} %get-tuple-element.38), channel_id=1, source_target_pairs={{0,7},{1,4},{2,5},{3,6},{4,3},{5,0},{6,1},{7,2},{8,15},{9,12},{10,... | collective-permute-start | bytes 479240 | tf_op jit(solution)/shard_map/ppermute | solution.py:538
  35.1 0.0 all-to-all-done.refs_0_
  35.1 2.8 %shard_map.92 = bf16[16,39,8,128]{3,2,1,0:T(8,128)(2,1)} custom-call(bf16[128,624]{1,0:T(8,128)(2,1)S(1)} %get-tuple-element.26.wide_ref, bf16[624,128]{1,0:T(8,128)(2,1)S(1)} %get-tuple-element.27.tall_ref, bf16[39,128,128]{2,1,0:T(8,128)(2,1)S(1)} %get-tuple-element.28.band_ref, bf16[8,39,16,128]{3,2,1,0:T(8,128)(2,1)S(1)} %all-to-all-done.refs_0_), custom_call_target="tpu_custom_call" | custom-call | flops 1000000000 | bytes 4000000 | tf_op jit(solution)/shard_map/pallas_call | solution.py:467
  37.9 0.0 copy-start.5
  37.9 11.0 %all-to-all-start.1 = ((bf16[16,39,8,128]{3,2,1,0:T(8,128)(2,1)}), bf16[16,39,8,128]{3,2,1,0:T(8,128)(2,1)S(1)}, u32[]{:S(2)}, u32[]{:S(2)}) async-start(bf16[16,39,8,128]{3,2,1,0:T(8,128)(2,1)} %shard_map.92), calls=%async_computation.1 | async-start | bytes 2555904 | tf_op jit(solution)/shard_map/all_to_all | solution.py:532
  48.9 0.0 collective-permute-done.2.refs_3_
  48.9 0.7 copy-done.6
  49.6 0.0 collective-permute-done.3.refs_4_
  49.6 0.0 collective-permute-done.4.refs_5_
  49.6 0.0 collective-permute-done.5.refs_6_
  49.6 0.0 collective-permute-done.6.refs_7_
  49.6 0.9 copy-done.7
  50.5 3.3 %shard_map.94 = (bf16[2,39,8,128]{3,2,1,0:T(8,128)(2,1)S(1)}, bf16[2,39,8,128]{3,2,1,0:T(8,128)(2,1)S(1)}, bf16[2,39,8,128]{3,2,1,0:T(8,128)(2,1)S(1)}, bf16[2,3...) custom-call(bf16[128,624]{1,0:T(8,128)(2,1)S(1)} %get-tuple-element., ...), custom_call_target="tpu_custom_call" | custom-call | flops 1000000000 | bytes 4000000 | tf_op jit(solution)/shard_map/pallas_call | solution.py:467
  53.9 0.0 copy-start.4
  53.9 2.9 %collective-permute-start.7 = (bf16[2,39,8,128]{3,2,1,0:T(8,128)(2,1)S(1)}, bf16[2,39,8,128]{3,2,1,0:T(8,128)(2,1)S(1)}, u32[]{:S(2)}, u32[]{:S(2)}) collective-permute-start(bf16[2,39,8,128]{3,2,1,0:T(8,128)(2,1)S(1)} %get-tuple-element.40), channel_id=1, source_target_pairs={{0,16},{8,24},{16,0},{24,8},{32,48},{40,56},{48,32},{56,40},{64,80... | collective-permute-start | bytes 479240 | tf_op jit(solution)/shard_map/ppermute | solution.py:554
  56.8 1.2 %collective-permute-start.8 = (bf16[2,39,8,128]{3,2,1,0:T(8,128)(2,1)S(1)}, bf16[2,39,8,128]{3,2,1,0:T(8,128)(2,1)S(1)}, u32[]{:S(2)}, u32[]{:S(2)}) collective-permute-start(bf16[2,39,8,128]{3,2,1,0:T(8,128)(2,1)S(1)} %get-tuple-element.41), channel_id=1, source_target_pairs={{0,32},{8,40},{16,48},{24,56},{32,64},{40,72},{48,80},{56,88},{64,... | collective-permute-start | bytes 479240 | tf_op jit(solution)/shard_map/ppermute | solution.py:554
  58.0 1.2 %collective-permute-start.9 = (bf16[2,39,8,128]{3,2,1,0:T(8,128)(2,1)S(1)}, bf16[2,39,8,128]{3,2,1,0:T(8,128)(2,1)S(1)}, u32[]{:S(2)}, u32[]{:S(2)}) collective-permute-start(bf16[2,39,8,128]{3,2,1,0:T(8,128)(2,1)S(1)} %get-tuple-element.42), channel_id=1, source_target_pairs={{0,48},{8,56},{16,32},{24,40},{32,80},{40,88},{48,64},{56,72},{64,... | collective-permute-start | bytes 479240 | tf_op jit(solution)/shard_map/ppermute | solution.py:554
  59.2 1.3 %collective-permute-start.10 = (bf16[2,39,8,128]{3,2,1,0:T(8,128)(2,1)S(1)}, bf16[2,39,8,128]{3,2,1,0:T(8,128)(2,1)S(1)}, u32[]{:S(2)}, u32[]{:S(2)}) collective-permute-start(bf16[2,39,8,128]{3,2,1,0:T(8,128)(2,1)S(1)} %get-tuple-element.43), channel_id=1, source_target_pairs={{0,64},{8,72},{16,80},{24,88},{32,96},{40,104},{48,112},{56,120},{... | collective-permute-start | bytes 479240 | tf_op jit(solution)/shard_map/ppermute | solution.py:554
  60.5 4.0 %collective-permute-start.11 = (bf16[2,39,8,128]{3,2,1,0:T(8,128)(2,1)S(1)}, bf16[2,39,8,128]{3,2,1,0:T(8,128)(2,1)S(1)}, u32[]{:S(2)}, u32[]{:S(2)}) collective-permute-start(bf16[2,39,8,128]{3,2,1,0:T(8,128)(2,1)S(1)} %get-tuple-element.44), channel_id=1, source_target_pairs={{0,80},{8,88},{16,64},{24,72},{32,112},{40,120},{48,96},{56,104},{... | collective-permute-start | bytes 479240 | tf_op jit(solution)/shard_map/ppermute | solution.py:554
  64.6 5.7 %collective-permute-done.7.refs_1_ = bf16[2,39,8,128]{3,2,1,0:T(8,128)(2,1)S(1)} collective-permute-done((bf16[2,39,8,128]{3,2,1,0:T(8,128)(2,1)S(1)}, bf16[2,39,8,128]{3,2,1,0:T(8,128)(2,1)S(1)}, u32[]{:S(2)}, u32[]{:S(2)}) %collective-permute-start.7) | collective-permute-done | bytes 159776 | tf_op jit(solution)/shard_map/ppermute | solution.py:554
  70.3 2.5 %collective-permute-start.12 = (bf16[2,39,8,128]{3,2,1,0:T(8,128)(2,1)S(1)}, bf16[2,39,8,128]{3,2,1,0:T(8,128)(2,1)S(1)}, u32[]{:S(2)}, u32[]{:S(2)}) collective-permute-start(bf16[2,39,8,128]{3,2,1,0:T(8,128)(2,1)S(1)} %get-tuple-element.45), channel_id=1, source_target_pairs={{0,96},{8,104},{16,112},{24,120},{32,0},{40,8},{48,16},{56,24},{64... | collective-permute-start | bytes 479240 | tf_op jit(solution)/shard_map/ppermute | solution.py:554
  72.8 1.1 %collective-permute-start.13 = (bf16[2,39,8,128]{3,2,1,0:T(8,128)(2,1)S(1)}, bf16[2,39,8,128]{3,2,1,0:T(8,128)(2,1)S(1)}, u32[]{:S(2)}, u32[]{:S(2)}) collective-permute-start(bf16[2,39,8,128]{3,2,1,0:T(8,128)(2,1)S(1)} %get-tuple-element.46), channel_id=1, source_target_pairs={{0,112},{8,120},{16,96},{24,104},{32,16},{40,24},{48,0},{56,8},{64... | collective-permute-start | bytes 479240 | tf_op jit(solution)/shard_map/ppermute | solution.py:554
  73.9 1.4 %collective-permute-done.9.refs_3_ = bf16[2,39,8,128]{3,2,1,0:T(8,128)(2,1)S(1)} collective-permute-done((bf16[2,39,8,128]{3,2,1,0:T(8,128)(2,1)S(1)}, bf16[2,39,8,128]{3,2,1,0:T(8,128)(2,1)S(1)}, u32[]{:S(2)}, u32[]{:S(2)}) %collective-permute-start.9) | collective-permute-done | bytes 159776 | tf_op jit(solution)/shard_map/ppermute | solution.py:554
  75.3 2.9 %collective-permute-done.10.refs_4_ = bf16[2,39,8,128]{3,2,1,0:T(8,128)(2,1)S(1)} collective-permute-done((bf16[2,39,8,128]{3,2,1,0:T(8,128)(2,1)S(1)}, bf16[2,39,8,128]{3,2,1,0:T(8,128)(2,1)S(1)}, u32[]{:S(2)}, u32[]{:S(2)}) %collective-permute-start.10) | collective-permute-done | bytes 159776 | tf_op jit(solution)/shard_map/ppermute | solution.py:554
  78.2 5.9 %collective-permute-done.11.refs_5_ = bf16[2,39,8,128]{3,2,1,0:T(8,128)(2,1)S(1)} collective-permute-done((bf16[2,39,8,128]{3,2,1,0:T(8,128)(2,1)S(1)}, bf16[2,39,8,128]{3,2,1,0:T(8,128)(2,1)S(1)}, u32[]{:S(2)}, u32[]{:S(2)}) %collective-permute-start.11) | collective-permute-done | bytes 159776 | tf_op jit(solution)/shard_map/ppermute | solution.py:554
  84.1 0.0 collective-permute-done.12.refs_6_
  84.1 0.0 collective-permute-done.13.refs_7_
  84.2 0.0 copy-start
  84.2 0.7 copy-done
  84.9 0.7 copy-done.2
  85.5 1.3 %collective-permute-start.14 = (bf16[8,39,8,128]{3,2,1,0:T(8,128)(2,1)S(1)}, bf16[8,39,8,128]{3,2,1,0:T(8,128)(2,1)S(1)}, u32[]{:S(2)}, u32[]{:S(2)}) collective-permute-start(bf16[8,39,8,128]{3,2,1,0:T(8,128)(2,1)S(1)} %forward.1), channel_id=1, source_target_pairs={{0,8},{8,0},{16,24},{24,16},{32,40},{40,32},{48,56},{56,48},{64,72... | collective-permute-start | bytes 1916936 | tf_op jit(solution)/shard_map/ppermute | solution.py:557
  86.8 0.0 all-to-all-done.1.values_ref
  86.8 1.3 %combine.1.first_ref = f32[39,8,128]{2,1,0:T(8,128)S(1)} custom-call(f32[16]{0:T(128)S(1)} %copy-done.4, bf16[16,39,8,128]{3,2,1,0:T(8,128)(2,1)S(1)} %all-to-all-done.1.values_ref), custom_call_target="tpu_custom_call" | custom-call | flops 10000000 | bytes 2000000 | tf_op jit(solution)/shard_map/combine/pallas_call | solution.py:494
  88.1 0.3 collective-permute-done.14.swapped_ref
  88.5 2.1 %finish.1 = f32[39,8,256]{2,1,0:T(8,128)} custom-call(f32[16]{0:T(128)S(1)} %copy-done.4, f32[39,8,128]{2,1,0:T(8,128)S(1)} %combine.1.first_ref, bf16[8,39,8,128]{3,2,1,0:T(8,128)(2,1)S(1)} %collective-permute-done.14.swapped_ref, bf16[2,39,8,128]{3,2,1,0:T(8,128)(2,1)S(1)} %get-tuple-element.39.refs_0_, ...), custom_call_target="tpu_custom_call" | custom-call | flops 10000000 | bytes 2000000 | tf_op jit(solution)/shard_map/finish/pallas_call | solution.py:506
  (18 shorter events, 0.1 us)
Async XLA Ops:
  4.6 30.5 %all-to-all-start = ((bf16[8,39,16,128]{3,2,1,0:T(8,128)(2,1)}), bf16[8,39,16,128]{3,2,1,0:T(8,128)(2,1)S(1)}, u32[]{:S(2)}, u32[]{:S(2)}) async-start(bf16[8,39,16,128]{3,2,1,0:T(8,128)(2,1)} %get-tuple-element.29), calls=%async_computation | async-start | bytes 2555904 | tf_op jit(solution)/shard_map/all_to_all | solution.py:532
  10.5 10.2 %copy-start.8 = (f32[39,16]{0,1:T(8,128)S(1)}, f32[39,16]{0,1:T(8,128)}, u32[]{:S(2)}) copy-start(f32[39,16]{0,1:T(8,128)} %param.13) | copy-start | bytes 7492
  10.5 10.2 %copy-start.9 = (bf16[8,39]{1,0:T(8,128)(2,1)S(1)}, bf16[8,39]{1,0:T(8,128)(2,1)}, u32[]{:S(2)}) copy-start(bf16[8,39]{1,0:T(8,128)(2,1)} %analysis_ref.1) | copy-start | bytes 1876
  10.5 10.2 %copy-start.10 = (bf16[39,8]{0,1:T(8,128)(2,1)S(1)}, bf16[39,8]{0,1:T(8,128)(2,1)}, u32[]{:S(2)}) copy-start(bf16[39,8]{0,1:T(8,128)(2,1)} %param.16) | copy-start | bytes 1876
  10.5 10.2 %copy-start.11 = (s32[39]{0:T(128)S(1)}, s32[39]{0:T(128)}, u32[]{:S(2)}) copy-start(s32[39]{0:T(128)} %refs_0_.1) | copy-start | bytes 472
  15.1 14.2 %collective-permute-start = (bf16[39,16,128]{2,1,0:T(8,128)(2,1)}, bf16[39,16,128]{2,1,0:T(8,128)(2,1)S(1)}, u32[]{:S(2)}, u32[]{:S(2)}) collective-permute-start(bf16[39,16,128]{2,1,0:T(8,128)(2,1)} %get-tuple-element.32), channel_id=1, source_target_pairs={{0,1},{1,2},{2,3},{3,0},{4,5},{5,6},{6,7},{7,4},{8,9},{9,10},{10,1... | collective-permute-start | bytes 479240 | tf_op jit(solution)/shard_map/ppermute | solution.py:538
  16.8 14.3 %collective-permute-start.1 = (bf16[39,16,128]{2,1,0:T(8,128)(2,1)}, bf16[39,16,128]{2,1,0:T(8,128)(2,1)S(1)}, u32[]{:S(2)}, u32[]{:S(2)}) collective-permute-start(bf16[39,16,128]{2,1,0:T(8,128)(2,1)} %get-tuple-element.33), channel_id=1, source_target_pairs={{0,2},{1,3},{2,0},{3,1},{4,6},{5,7},{6,4},{7,5},{8,10},{9,11},{10,... | collective-permute-start | bytes 479240 | tf_op jit(solution)/shard_map/ppermute | solution.py:538
  17.3 31.6 %collective-permute-start.2 = (bf16[39,16,128]{2,1,0:T(8,128)(2,1)}, bf16[39,16,128]{2,1,0:T(8,128)(2,1)S(1)}, u32[]{:S(2)}, u32[]{:S(2)}) collective-permute-start(bf16[39,16,128]{2,1,0:T(8,128)(2,1)} %get-tuple-element.34), channel_id=1, source_target_pairs={{0,3},{1,0},{2,1},{3,2},{4,7},{5,4},{6,5},{7,6},{8,11},{9,8},{10,9... | collective-permute-start | bytes 479240 | tf_op jit(solution)/shard_map/ppermute | solution.py:538
  19.2 30.4 %collective-permute-start.3 = (bf16[39,16,128]{2,1,0:T(8,128)(2,1)}, bf16[39,16,128]{2,1,0:T(8,128)(2,1)}, u32[]{:S(2)}, u32[]{:S(2)}) collective-permute-start(bf16[39,16,128]{2,1,0:T(8,128)(2,1)} %get-tuple-element.35), channel_id=1, source_target_pairs={{0,4},{1,5},{2,6},{3,7},{4,0},{5,1},{6,2},{7,3},{8,12},{9,13},{10,... | collective-permute-start | bytes 479240 | tf_op jit(solution)/shard_map/ppermute | solution.py:538
  20.7 28.9 %collective-permute-start.4 = (bf16[39,16,128]{2,1,0:T(8,128)(2,1)}, bf16[39,16,128]{2,1,0:T(8,128)(2,1)}, u32[]{:S(2)}, u32[]{:S(2)}) collective-permute-start(bf16[39,16,128]{2,1,0:T(8,128)(2,1)} %get-tuple-element.36), channel_id=1, source_target_pairs={{0,5},{1,6},{2,7},{3,4},{4,1},{5,2},{6,3},{7,0},{8,13},{9,14},{10,... | collective-permute-start | bytes 479240 | tf_op jit(solution)/shard_map/ppermute | solution.py:538
  29.3 20.3 %collective-permute-start.5 = (bf16[39,16,128]{2,1,0:T(8,128)(2,1)}, bf16[39,16,128]{2,1,0:T(8,128)(2,1)}, u32[]{:S(2)}, u32[]{:S(2)}) collective-permute-start(bf16[39,16,128]{2,1,0:T(8,128)(2,1)} %get-tuple-element.37), channel_id=1, source_target_pairs={{0,6},{1,7},{2,4},{3,5},{4,2},{5,3},{6,0},{7,1},{8,14},{9,15},{10,... | collective-permute-start | bytes 479240 | tf_op jit(solution)/shard_map/ppermute | solution.py:538
  31.1 18.5 %collective-permute-start.6 = (bf16[39,16,128]{2,1,0:T(8,128)(2,1)}, bf16[39,16,128]{2,1,0:T(8,128)(2,1)}, u32[]{:S(2)}, u32[]{:S(2)}) collective-permute-start(bf16[39,16,128]{2,1,0:T(8,128)(2,1)} %get-tuple-element.38), channel_id=1, source_target_pairs={{0,7},{1,4},{2,5},{3,6},{4,3},{5,0},{6,1},{7,2},{8,15},{9,12},{10,... | collective-permute-start | bytes 479240 | tf_op jit(solution)/shard_map/ppermute | solution.py:538
  37.9 11.7 %copy-start.5 = (bf16[39,16,128]{2,1,0:T(8,128)(2,1)S(1)}, bf16[39,16,128]{2,1,0:T(8,128)(2,1)}, u32[]{:S(2)}) copy-start(bf16[39,16,128]{2,1,0:T(8,128)(2,1)} %get-tuple-element.31.refs_0_) | copy-start | bytes 479236
  37.9 48.9 %all-to-all-start.1 = ((bf16[16,39,8,128]{3,2,1,0:T(8,128)(2,1)}), bf16[16,39,8,128]{3,2,1,0:T(8,128)(2,1)S(1)}, u32[]{:S(2)}, u32[]{:S(2)}) async-start(bf16[16,39,8,128]{3,2,1,0:T(8,128)(2,1)} %shard_map.92), calls=%async_computation.1 | async-start | bytes 2555904 | tf_op jit(solution)/shard_map/all_to_all | solution.py:532
  48.9 0.7 copy-start.6
  49.6 0.9 %copy-start.7 = (bf16[39,16,128]{2,1,0:T(8,128)(2,1)S(1)}, bf16[39,16,128]{2,1,0:T(8,128)(2,1)}, u32[]{:S(2)}) copy-start(bf16[39,16,128]{2,1,0:T(8,128)(2,1)} %copy-done.6) | copy-start | bytes 479236
  53.9 32.9 %copy-start.4 = (f32[16]{0:T(128)S(1)}, f32[16]{0:T(128)}, u32[]{:S(2)}) copy-start(f32[16]{0:T(128)} %weights_ref.3) | copy-start | bytes 196
  53.9 16.4 %collective-permute-start.7 = (bf16[2,39,8,128]{3,2,1,0:T(8,128)(2,1)S(1)}, bf16[2,39,8,128]{3,2,1,0:T(8,128)(2,1)S(1)}, u32[]{:S(2)}, u32[]{:S(2)}) collective-permute-start(bf16[2,39,8,128]{3,2,1,0:T(8,128)(2,1)S(1)} %get-tuple-element.40), channel_id=1, source_target_pairs={{0,16},{8,24},{16,0},{24,8},{32,48},{40,56},{48,32},{56,40},{64,80... | collective-permute-start | bytes 479240 | tf_op jit(solution)/shard_map/ppermute | solution.py:554
  56.8 16.0 %collective-permute-start.8 = (bf16[2,39,8,128]{3,2,1,0:T(8,128)(2,1)S(1)}, bf16[2,39,8,128]{3,2,1,0:T(8,128)(2,1)S(1)}, u32[]{:S(2)}, u32[]{:S(2)}) collective-permute-start(bf16[2,39,8,128]{3,2,1,0:T(8,128)(2,1)S(1)} %get-tuple-element.41), channel_id=1, source_target_pairs={{0,32},{8,40},{16,48},{24,56},{32,64},{40,72},{48,80},{56,88},{64,... | collective-permute-start | bytes 479240 | tf_op jit(solution)/shard_map/ppermute | solution.py:554
  58.0 17.3 %collective-permute-start.9 = (bf16[2,39,8,128]{3,2,1,0:T(8,128)(2,1)S(1)}, bf16[2,39,8,128]{3,2,1,0:T(8,128)(2,1)S(1)}, u32[]{:S(2)}, u32[]{:S(2)}) collective-permute-start(bf16[2,39,8,128]{3,2,1,0:T(8,128)(2,1)S(1)} %get-tuple-element.42), channel_id=1, source_target_pairs={{0,48},{8,56},{16,32},{24,40},{32,80},{40,88},{48,64},{56,72},{64,... | collective-permute-start | bytes 479240 | tf_op jit(solution)/shard_map/ppermute | solution.py:554
  59.2 19.0 %collective-permute-start.10 = (bf16[2,39,8,128]{3,2,1,0:T(8,128)(2,1)S(1)}, bf16[2,39,8,128]{3,2,1,0:T(8,128)(2,1)S(1)}, u32[]{:S(2)}, u32[]{:S(2)}) collective-permute-start(bf16[2,39,8,128]{3,2,1,0:T(8,128)(2,1)S(1)} %get-tuple-element.43), channel_id=1, source_target_pairs={{0,64},{8,72},{16,80},{24,88},{32,96},{40,104},{48,112},{56,120},{... | collective-permute-start | bytes 479240 | tf_op jit(solution)/shard_map/ppermute | solution.py:554
  60.5 23.6 %collective-permute-start.11 = (bf16[2,39,8,128]{3,2,1,0:T(8,128)(2,1)S(1)}, bf16[2,39,8,128]{3,2,1,0:T(8,128)(2,1)S(1)}, u32[]{:S(2)}, u32[]{:S(2)}) collective-permute-start(bf16[2,39,8,128]{3,2,1,0:T(8,128)(2,1)S(1)} %get-tuple-element.44), channel_id=1, source_target_pairs={{0,80},{8,88},{16,64},{24,72},{32,112},{40,120},{48,96},{56,104},{... | collective-permute-start | bytes 479240 | tf_op jit(solution)/shard_map/ppermute | solution.py:554
  70.3 13.8 %collective-permute-start.12 = (bf16[2,39,8,128]{3,2,1,0:T(8,128)(2,1)S(1)}, bf16[2,39,8,128]{3,2,1,0:T(8,128)(2,1)S(1)}, u32[]{:S(2)}, u32[]{:S(2)}) collective-permute-start(bf16[2,39,8,128]{3,2,1,0:T(8,128)(2,1)S(1)} %get-tuple-element.45), channel_id=1, source_target_pairs={{0,96},{8,104},{16,112},{24,120},{32,0},{40,8},{48,16},{56,24},{64... | collective-permute-start | bytes 479240 | tf_op jit(solution)/shard_map/ppermute | solution.py:554
  72.8 11.4 %collective-permute-start.13 = (bf16[2,39,8,128]{3,2,1,0:T(8,128)(2,1)S(1)}, bf16[2,39,8,128]{3,2,1,0:T(8,128)(2,1)S(1)}, u32[]{:S(2)}, u32[]{:S(2)}) collective-permute-start(bf16[2,39,8,128]{3,2,1,0:T(8,128)(2,1)S(1)} %get-tuple-element.46), channel_id=1, source_target_pairs={{0,112},{8,120},{16,96},{24,104},{32,16},{40,24},{48,0},{56,8},{64... | collective-permute-start | bytes 479240 | tf_op jit(solution)/shard_map/ppermute | solution.py:554
  84.2 0.7 copy-start
  84.9 0.7 copy-start.2
  85.5 3.0 %collective-permute-start.14 = (bf16[8,39,8,128]{3,2,1,0:T(8,128)(2,1)S(1)}, bf16[8,39,8,128]{3,2,1,0:T(8,128)(2,1)S(1)}, u32[]{:S(2)}, u32[]{:S(2)}) collective-permute-start(bf16[8,39,8,128]{3,2,1,0:T(8,128)(2,1)S(1)} %forward.1), channel_id=1, source_target_pairs={{0,8},{8,0},{16,24},{24,16},{32,40},{40,32},{48,56},{56,48},{64,72... | collective-permute-start | bytes 1916936 | tf_op jit(solution)/shard_map/ppermute | solution.py:557
  86.8 1.7 %copy-start.1 = (bf16[2,39,8,128]{3,2,1,0:T(8,128)(2,1)S(1)}, bf16[2,39,8,128]{3,2,1,0:T(8,128)(2,1)}, u32[]{:S(2)}) copy-start(bf16[2,39,8,128]{3,2,1,0:T(8,128)(2,1)} %copy-done) | copy-start | bytes 479236
  86.8 1.7 %copy-start.3 = (bf16[2,39,8,128]{3,2,1,0:T(8,128)(2,1)S(1)}, bf16[2,39,8,128]{3,2,1,0:T(8,128)(2,1)}, u32[]{:S(2)}) copy-start(bf16[2,39,8,128]{3,2,1,0:T(8,128)(2,1)} %copy-done.2) | copy-start | bytes 479236

commit v4 on v3

--- a/solution.py
+++ b/solution.py
@@ -12,7 +12,9 @@
 NEAR = 64
 GROUPS = 3
 RING = 4
-GRANT = 20 * 2**20
+ROW_ORDER = (4, 1, 3, 6, 5, 7, 2, 0)
+CHIP_ORDER = (5, 4, 3, 7, 2, 6, 1, 0)
+GRANT = 8 * 2**20
 VMEM = pl.BlockSpec(memory_space=pltpu.VMEM)
 SMEM = pl.BlockSpec(memory_space=pltpu.SMEM)
 ANY = pl.BlockSpec(memory_space=pl.ANY)
@@ -31,10 +33,12 @@
 
 
 def partner(me, step, sign):
+    step = ROW_ORDER[step]
     return (me // RING ^ step // RING) * RING + (me + sign * step) % RING
 
 
 def chip_partner(chip, step, sign):
+    step = CHIP_ORDER[step]
     return (chip // 2 + sign * (step // 2)) % RING * 2 + (chip % 2 ^ step % 2)
 
 
@@ -221,7 +225,8 @@
             copy.start()
         return carry
 
-    lax.fori_loop(0, GROUPS, work, 0)
+    for group in range(GROUPS):
+        work(group, 0)
     for group in range(GROUPS):
         for copy in saves(group):
             copy.wait()
@@ -301,7 +306,8 @@
                 resampled_ref[part, channel] = result[part * part_rows : (part + 1) * part_rows]
         return carry
 
-    lax.fori_loop(0, GROUPS, work, 0)
+    for group in range(GROUPS):
+        work(group, 0)
     owned = done_ref.shape[2]
     long = tall_ref.shape[0]
     steps = parts // 2
@@ -343,10 +349,11 @@
 
 
 def forward_kernel(*refs):
-    given, kept_ref = refs[:-1], refs[-1]
-    other = 1 - lax.axis_index("exp") % 2
+    given, (own_ref, other_ref) = refs[:-2], refs[-2:]
+    core = lax.axis_index("exp") % 2
     for index, ref in enumerate(given):
-        kept_ref[index] = ref[other]
+        own_ref[index] = ref[core]
+        other_ref[index] = ref[1 - core]
 
 
 def combine_channel(sources, channel):
@@ -366,12 +373,22 @@
     return weighted / jnp.sqrt(total * spread)
 
 
-def combine_kernel(weights_ref, values_ref, map_ref):
-    channels = map_ref.shape[0]
-    size = channels // GROUPS
-    sources = [
-        (values_ref, index, weights_ref[index]) for index in range(values_ref.shape[0])
-    ]
+def sources_of(weights_ref, refs):
+    if len(refs) == 1:
+        return [(refs[0], index, weights_ref[index]) for index in range(refs[0].shape[0])]
+    me = lax.axis_index("exp")
+    sources = []
+    for step in range(refs[0].shape[0]):
+        chip = chip_partner(me // 2, step, -1)
+        sources.append((refs[0], step, weights_ref[2 * chip + me % 2]))
+        sources.append((refs[1], step, weights_ref[2 * chip + 1 - me % 2]))
+    return sources
+
+
+def combine_kernel(weights_ref, *refs):
+    values_refs, map_ref = refs[:-1], refs[-1]
+    size = map_ref.shape[0] // GROUPS
+    sources = sources_of(weights_ref, values_refs)
 
     def work(group, carry):
         for index in range(size):
@@ -381,17 +398,11 @@
     lax.fori_loop(0, GROUPS, work, 0)
 
 
-def finish_kernel(weights_ref, first_ref, swapped_ref, *refs):
-    kept_refs, (map_ref, held_ref, sems) = refs[:-3], refs[-3:]
-    channels = held_ref.shape[0]
-    size = channels // GROUPS
-    me = lax.axis_index("exp")
-    core = me % 2
-    sources = []
-    for step, ref in enumerate(kept_refs):
-        chip = chip_partner(me // 2, step, -1)
-        sources.append((ref, core, weights_ref[2 * chip + core]))
-        sources.append((swapped_ref, step, weights_ref[2 * chip + 1 - core]))
+def finish_kernel(other_half, weights_ref, ready_ref, *refs):
+    values_refs, (map_ref, held_ref, sems) = refs[:-3], refs[-3:]
+    size = held_ref.shape[0] // GROUPS
+    sources = sources_of(weights_ref, values_refs)
+    columns = [slice(0, LANES), slice(LANES, 2 * LANES)]
 
     def save(group):
         span = pl.ds(group * size, size)
@@ -400,8 +411,8 @@
     def work(group, carry):
         for index in range(size):
             channel = group * size + index
-            held_ref[channel, :, :LANES] = first_ref[channel]
-            held_ref[channel, :, LANES:] = combine_channel(sources, channel)
+            held_ref[channel, :, columns[other_half]] = ready_ref[channel]
+            held_ref[channel, :, columns[1 - other_half]] = combine_channel(sources, channel)
         save(group).start()
         return carry
 
@@ -482,37 +493,37 @@
     def forward(given):
         return pl.pallas_call(
             forward_kernel,
-            out_shape=jax.ShapeDtypeStruct((len(given),) + out_shape[1:], bf16),
+            out_shape=[jax.ShapeDtypeStruct((len(given),) + out_shape[1:], bf16)] * 2,
             in_specs=[VMEM] * len(given),
-            out_specs=VMEM,
+            out_specs=[VMEM] * 2,
             compiler_params=pltpu.CompilerParams(vmem_limit_bytes=GRANT),
             cost_estimate=estimate(0, 2 * 10**6),
             name="forward",
         )(*given)
 
-    def combine(gathered):
+    def combine(*values):
         return pl.pallas_call(
             combine_kernel,
             out_shape=jax.ShapeDtypeStruct(out_shape[1:], jnp.float32),
-            in_specs=[SMEM, VMEM],
+            in_specs=[SMEM] + [VMEM] * len(values),
             out_specs=VMEM,
             compiler_params=pltpu.CompilerParams(vmem_limit_bytes=GRANT),
             cost_estimate=estimate(10**7, 2 * 10**6),
             name="combine",
-        )(exposure_weights, gathered)
-
-    def finish(first, swapped, kept):
+        )(exposure_weights, *values)
+
+    def finish(other_half, ready, *values):
         shape = (channels, owned, 2 * LANES)
         return pl.pallas_call(
-            finish_kernel,
+            functools.partial(finish_kernel, other_half),
             out_shape=jax.ShapeDtypeStruct(shape, jnp.float32),
-            in_specs=[SMEM] + [VMEM] * (2 + len(kept)),
+            in_specs=[SMEM] + [VMEM] * (1 + len(values)),
             out_specs=ANY,
             scratch_shapes=[pltpu.VMEM(shape, jnp.float32), dma((GROUPS,))],
             compiler_params=pltpu.CompilerParams(vmem_limit_bytes=GRANT),
             cost_estimate=estimate(10**7, 2 * 10**6),
             name="finish",
-        )(exposure_weights, first, swapped, *kept)
+        )(exposure_weights, ready, *values)
 
     band, wide, tall = pl.pallas_call(
         prepare_kernel,
@@ -532,7 +543,7 @@
         return lax.all_to_all(value, axis, split_axis=0, concat_axis=0, tiled=True)
 
     def shift(value, step):
-        if step == 0:
+        if ROW_ORDER[step] == 0:
             return value
         pairs = [(me, int(partner(me, step, 1))) for me in range(row_parts)]
         return lax.ppermute(value, "row", pairs)
@@ -546,7 +557,7 @@
     pieces = resample_rows(exp_parts // 2, band, wide, tall, columns[1])
 
     def pass_on(value, step):
-        if step == 0:
+        if CHIP_ORDER[step] == 0:
             return value
         pairs = [
             (me, int(chip_partner(me // 2, step, 1)) * 2 + me % 2) for me in range(exp_parts)
@@ -554,8 +565,9 @@
         return lax.ppermute(value, "exp", pairs)
 
     kept = [pass_on(value, step) for step, value in enumerate(pieces)]
-    swapped = lax.ppermute(forward(kept), "exp", [(me, me ^ 1) for me in range(exp_parts)])
-    return finish(combine(gathered), swapped, kept)
+    own, other = forward(kept)
+    swapped = lax.ppermute(other, "exp", [(me, me ^ 1) for me in range(exp_parts)])
+    return finish(0, combine(gathered), own, swapped)
 
 
 def solution(mesh):

time: 91 us -> 87.1 us (0.957)
  the two profiles are of different devices: /device:TPU:3 before, /device:TPU:1 now
where the time goes in v4:
time: 87.1 us; the launch traced here: 86.7 us
  starting transfers between devices  40.8 us (47%)
  waiting for transfers between devices  25.3 us (29%)
  Pallas kernels  20.5 us (24%)
    ppermute x7, waiting for transfers between devices, pass_on(): return lax.ppermute(value, 'exp', pairs)  18.5 us
    all_to_all x2, starting transfers between devices, exchange(): return lax.all_to_all(value, axis, split_axis=0, concat_axis=0, tiled=True)  14.9 us
    ppermute x7, starting transfers between devices, pass_on(): return lax.ppermute(value, 'exp', pairs)  14.3 us
    ppermute x7, starting transfers between devices, shift(): return lax.ppermute(value, 'row', pairs)  11 us
    pallas_call x2, Pallas kernels, resample_columns(): pl.pallas_call(functools.partial(columns_kernel, half, count), out_shape=...  9.5 us
    ppermute x7, waiting for transfers between devices, shift(): return lax.ppermute(value, 'row', pairs)  6.36 us
    pallas_call x2, Pallas kernels, resample_rows(): pl.pallas_call(functools.partial(rows_kernel, count, chips), out_shape=[j...  5.48 us
    pallas_call x1, Pallas kernels, program(): pl.pallas_call(prepare_kernel, out_shape=[jax.ShapeDtypeStruct((channels,...  2.07 us
  transfers between devices with their start and end apart: 17, of which 8 were waited for; matrix products, arithmetic and copies ran while one was open for 0% of the time, Pallas kernels for 16%

profile of v4, /device:TPU:1, one launch (start us, length us, event | category | flops | bytes accessed | tf_op | source)
XLA Modules:
  0.0 86.7 jit_solution(13356900169400278108)
XLA Ops:
  0.0 4.7 %shard_map.91 = (bf16[8,39,16,128]{3,2,1,0:T(8,128)(2,1)}, bf16[39,128,128]{2,1,0:T(8,128)(2,1)}) custom-call(s32[16]{0:T(128)} %rows_ref.3, s32[16]{0:T(128)} %cols_ref.3, f32[1,16,39]{2,1,0:T(8,128)} %bitcast.9, bf16[39,16,2048]{2,1,0:T(8,128)(2,1)} %bitcast.7, s32[39]{0:T(128)} %refs_0_.1, f32[16,39]{1,0:T(8,128)} %bitcast.4), custom_call_target="tpu_custom_call" | custom-call | flops 1000000000 | bytes 4000000 | tf_op jit(solution)/shard_map/pallas_call | solution.py:456
  4.7 6.1 %all-to-all-start = ((bf16[8,39,16,128]{3,2,1,0:T(8,128)(2,1)}), bf16[8,39,16,128]{3,2,1,0:T(8,128)(2,1)S(1)}, u32[]{:S(2)}, u32[]{:S(2)}) async-start(bf16[8,39,16,128]{3,2,1,0:T(8,128)(2,1)} %get-tuple-element.31), calls=%async_computation | async-start | bytes 2555904 | tf_op jit(solution)/shard_map/all_to_all | solution.py:543
  10.8 0.0 copy-start.3
  10.8 0.0 copy-start.4
  10.9 0.0 copy-start.5
  10.9 4.8 %shard_map.93 = (bf16[39,16,128]{2,1,0:T(8,128)(2,1)}, bf16[39,16,128]{2,1,0:T(8,128)(2,1)}, bf16[39,16,128]{2,1,0:T(8,128)(2,1)}, bf16[39,16,128]{2,1,0:T(8,128...) custom-call(s32[16]{0:T(128)} %rows_ref.3, ...), custom_call_target="tpu_custom_call" | custom-call | flops 1000000000 | bytes 4000000 | tf_op jit(solution)/shard_map/pallas_call | solution.py:456
  15.6 1.2 %collective-permute-start = (bf16[39,16,128]{2,1,0:T(8,128)(2,1)}, bf16[39,16,128]{2,1,0:T(8,128)(2,1)S(1)}, u32[]{:S(2)}, u32[]{:S(2)}) collective-permute-start(bf16[39,16,128]{2,1,0:T(8,128)(2,1)} %get-tuple-element.33), channel_id=1, source_target_pairs={{0,4},{1,5},{2,6},{3,7},{4,0},{5,1},{6,2},{7,3},{8,12},{9,13},{10,... | collective-permute-start | bytes 479240 | tf_op jit(solution)/shard_map/ppermute | solution.py:549
  16.8 1.3 %collective-permute-start.1 = (bf16[39,16,128]{2,1,0:T(8,128)(2,1)}, bf16[39,16,128]{2,1,0:T(8,128)(2,1)S(1)}, u32[]{:S(2)}, u32[]{:S(2)}) collective-permute-start(bf16[39,16,128]{2,1,0:T(8,128)(2,1)} %get-tuple-element.34), channel_id=1, source_target_pairs={{0,1},{1,2},{2,3},{3,0},{4,5},{5,6},{6,7},{7,4},{8,9},{9,10},{10,1... | collective-permute-start | bytes 479240 | tf_op jit(solution)/shard_map/ppermute | solution.py:549
  18.1 1.6 %collective-permute-start.2 = (bf16[39,16,128]{2,1,0:T(8,128)(2,1)}, bf16[39,16,128]{2,1,0:T(8,128)(2,1)S(1)}, u32[]{:S(2)}, u32[]{:S(2)}) collective-permute-start(bf16[39,16,128]{2,1,0:T(8,128)(2,1)} %get-tuple-element.35), channel_id=1, source_target_pairs={{0,3},{1,0},{2,1},{3,2},{4,7},{5,4},{6,5},{7,6},{8,11},{9,8},{10,9... | collective-permute-start | bytes 479240 | tf_op jit(solution)/shard_map/ppermute | solution.py:549
  19.7 1.7 %collective-permute-start.3 = (bf16[39,16,128]{2,1,0:T(8,128)(2,1)}, bf16[39,16,128]{2,1,0:T(8,128)(2,1)}, u32[]{:S(2)}, u32[]{:S(2)}) collective-permute-start(bf16[39,16,128]{2,1,0:T(8,128)(2,1)} %get-tuple-element.36), channel_id=1, source_target_pairs={{0,6},{1,7},{2,4},{3,5},{4,2},{5,3},{6,0},{7,1},{8,14},{9,15},{10,... | collective-permute-start | bytes 479240 | tf_op jit(solution)/shard_map/ppermute | solution.py:549
  21.4 1.2 %collective-permute-start.4 = (bf16[39,16,128]{2,1,0:T(8,128)(2,1)}, bf16[39,16,128]{2,1,0:T(8,128)(2,1)}, u32[]{:S(2)}, u32[]{:S(2)}) collective-permute-start(bf16[39,16,128]{2,1,0:T(8,128)(2,1)} %get-tuple-element.37), channel_id=1, source_target_pairs={{0,5},{1,6},{2,7},{3,4},{4,1},{5,2},{6,3},{7,0},{8,13},{9,14},{10,... | collective-permute-start | bytes 479240 | tf_op jit(solution)/shard_map/ppermute | solution.py:549
  22.6 0.0 copy-done.2
  22.6 2.1 %prepare.1 = (bf16[39,128,128]{2,1,0:T(8,128)(2,1)S(1)}, bf16[128,624]{1,0:T(8,128)(2,1)S(1)}, bf16[624,128]{1,0:T(8,128)(2,1)S(1)}) custom-call(s32[39]{0:T(128)S(1)} %copy-done.5, f32[16,39]{1,0:T(8,128)S(1)} %bitcast.5, bf16[8,39]{1,0:T(8,128)(2,1)S(1)} %copy-done.3, bf16[8,39]{1,0:T(8,128)(2,1)S(1)} %bitcast.6), custom_call_target="tpu_custom_call" | custom-call | flops 10000000 | bytes 2000000 | tf_op jit(solution)/shard_map/prepare/pallas_call | solution.py:528
  24.7 6.3 %collective-permute-done.refs_0_ = bf16[39,16,128]{2,1,0:T(8,128)(2,1)S(1)} collective-permute-done((bf16[39,16,128]{2,1,0:T(8,128)(2,1)}, bf16[39,16,128]{2,1,0:T(8,128)(2,1)S(1)}, u32[]{:S(2)}, u32[]{:S(2)}) %collective-permute-start) | collective-permute-done | bytes 159776 | tf_op jit(solution)/shard_map/ppermute | solution.py:549
  31.1 1.9 %collective-permute-start.5 = (bf16[39,16,128]{2,1,0:T(8,128)(2,1)}, bf16[39,16,128]{2,1,0:T(8,128)(2,1)}, u32[]{:S(2)}, u32[]{:S(2)}) collective-permute-start(bf16[39,16,128]{2,1,0:T(8,128)(2,1)} %get-tuple-element.38), channel_id=1, source_target_pairs={{0,7},{1,4},{2,5},{3,6},{4,3},{5,0},{6,1},{7,2},{8,15},{9,12},{10,... | collective-permute-start | bytes 479240 | tf_op jit(solution)/shard_map/ppermute | solution.py:549
  33.0 0.0 collective-permute-done.1.refs_1_
  33.0 2.1 %collective-permute-start.6 = (bf16[39,16,128]{2,1,0:T(8,128)(2,1)}, bf16[39,16,128]{2,1,0:T(8,128)(2,1)}, u32[]{:S(2)}, u32[]{:S(2)}) collective-permute-start(bf16[39,16,128]{2,1,0:T(8,128)(2,1)} %get-tuple-element.39), channel_id=1, source_target_pairs={{0,2},{1,3},{2,0},{3,1},{4,6},{5,7},{6,4},{7,5},{8,10},{9,11},{10,... | collective-permute-start | bytes 479240 | tf_op jit(solution)/shard_map/ppermute | solution.py:549
  35.1 0.0 all-to-all-done.refs_0_
  35.1 2.4 %shard_map.92 = bf16[16,39,8,128]{3,2,1,0:T(8,128)(2,1)} custom-call(bf16[128,624]{1,0:T(8,128)(2,1)S(1)} %get-tuple-element.28.wide_ref, bf16[624,128]{1,0:T(8,128)(2,1)S(1)} %get-tuple-element.29.tall_ref, bf16[39,128,128]{2,1,0:T(8,128)(2,1)S(1)} %get-tuple-element.30.band_ref, bf16[8,39,16,128]{3,2,1,0:T(8,128)(2,1)S(1)} %all-to-all-done.refs_0_), custom_call_target="tpu_custom_call" | custom-call | flops 1000000000 | bytes 4000000 | tf_op jit(solution)/shard_map/pallas_call | solution.py:478
  37.5 0.0 copy-start.1
  37.5 8.8 %all-to-all-start.1 = ((bf16[16,39,8,128]{3,2,1,0:T(8,128)(2,1)}), bf16[16,39,8,128]{3,2,1,0:T(8,128)(2,1)S(1)}, u32[]{:S(2)}, u32[]{:S(2)}) async-start(bf16[16,39,8,128]{3,2,1,0:T(8,128)(2,1)} %shard_map.92), calls=%async_computation.1 | async-start | bytes 2555904 | tf_op jit(solution)/shard_map/all_to_all | solution.py:543
  46.3 0.0 collective-permute-done.2.refs_2_
  46.3 0.0 collective-permute-done.3.refs_3_
  46.3 0.0 collective-permute-done.4.refs_4_
  46.3 0.0 collective-permute-done.5.refs_5_
  46.4 0.0 collective-permute-done.6.refs_6_
  46.4 3.1 %shard_map.94 = (bf16[2,39,8,128]{3,2,1,0:T(8,128)(2,1)S(1)}, bf16[2,39,8,128]{3,2,1,0:T(8,128)(2,1)S(1)}, bf16[2,39,8,128]{3,2,1,0:T(8,128)(2,1)S(1)}, bf16[2,3...) custom-call(bf16[128,624]{1,0:T(8,128)(2,1)S(1)} %get-tuple-element., ...), custom_call_target="tpu_custom_call" | custom-call | flops 1000000000 | bytes 4000000 | tf_op jit(solution)/shard_map/pallas_call | solution.py:478
  49.4 0.0 copy-start
  49.5 5.3 %collective-permute-start.7 = (bf16[2,39,8,128]{3,2,1,0:T(8,128)(2,1)S(1)}, bf16[2,39,8,128]{3,2,1,0:T(8,128)(2,1)S(1)}, u32[]{:S(2)}, u32[]{:S(2)}) collective-permute-start(bf16[2,39,8,128]{3,2,1,0:T(8,128)(2,1)S(1)} %get-tuple-element.41), channel_id=1, source_target_pairs={{0,80},{8,88},{16,64},{24,72},{32,112},{40,120},{48,96},{56,104},{... | collective-permute-start | bytes 479240 | tf_op jit(solution)/shard_map/ppermute | solution.py:565
  54.8 0.3 collective-permute-start.8
  55.1 1.2 %collective-permute-start.9 = (bf16[2,39,8,128]{3,2,1,0:T(8,128)(2,1)S(1)}, bf16[2,39,8,128]{3,2,1,0:T(8,128)(2,1)S(1)}, u32[]{:S(2)}, u32[]{:S(2)}) collective-permute-start(bf16[2,39,8,128]{3,2,1,0:T(8,128)(2,1)S(1)} %get-tuple-element.43), channel_id=1, source_target_pairs={{0,48},{8,56},{16,32},{24,40},{32,80},{40,88},{48,64},{56,72},{64,... | collective-permute-start | bytes 479240 | tf_op jit(solution)/shard_map/ppermute | solution.py:565
  56.3 3.9 %collective-permute-start.10 = (bf16[2,39,8,128]{3,2,1,0:T(8,128)(2,1)S(1)}, bf16[2,39,8,128]{3,2,1,0:T(8,128)(2,1)S(1)}, u32[]{:S(2)}, u32[]{:S(2)}) collective-permute-start(bf16[2,39,8,128]{3,2,1,0:T(8,128)(2,1)S(1)} %get-tuple-element.44), channel_id=1, source_target_pairs={{0,112},{8,120},{16,96},{24,104},{32,16},{40,24},{48,0},{56,8},{64... | collective-permute-start | bytes 479240 | tf_op jit(solution)/shard_map/ppermute | solution.py:565
  60.2 0.0 collective-permute-start.11
  60.2 9.5 %collective-permute-done.7.refs_0_ = bf16[2,39,8,128]{3,2,1,0:T(8,128)(2,1)S(1)} collective-permute-done((bf16[2,39,8,128]{3,2,1,0:T(8,128)(2,1)S(1)}, bf16[2,39,8,128]{3,2,1,0:T(8,128)(2,1)S(1)}, u32[]{:S(2)}, u32[]{:S(2)}) %collective-permute-start.7) | collective-permute-done | bytes 159776 | tf_op jit(solution)/shard_map/ppermute | solution.py:565
  69.7 1.2 %collective-permute-start.12 = (bf16[2,39,8,128]{3,2,1,0:T(8,128)(2,1)S(1)}, bf16[2,39,8,128]{3,2,1,0:T(8,128)(2,1)S(1)}, u32[]{:S(2)}, u32[]{:S(2)}) collective-permute-start(bf16[2,39,8,128]{3,2,1,0:T(8,128)(2,1)S(1)} %get-tuple-element.46), channel_id=1, source_target_pairs={{0,96},{8,104},{16,112},{24,120},{32,0},{40,8},{48,16},{56,24},{64... | collective-permute-start | bytes 479240 | tf_op jit(solution)/shard_map/ppermute | solution.py:565
  70.8 0.1 collective-permute-done.8.refs_1_
  71.0 2.4 %collective-permute-start.13 = (bf16[2,39,8,128]{3,2,1,0:T(8,128)(2,1)S(1)}, bf16[2,39,8,128]{3,2,1,0:T(8,128)(2,1)S(1)}, u32[]{:S(2)}, u32[]{:S(2)}) collective-permute-start(bf16[2,39,8,128]{3,2,1,0:T(8,128)(2,1)S(1)} %get-tuple-element.47), channel_id=1, source_target_pairs={{0,16},{8,24},{16,0},{24,8},{32,48},{40,56},{48,32},{56,40},{64,80... | collective-permute-start | bytes 479240 | tf_op jit(solution)/shard_map/ppermute | solution.py:565
  73.4 4.2 %collective-permute-done.9.refs_2_ = bf16[2,39,8,128]{3,2,1,0:T(8,128)(2,1)S(1)} collective-permute-done((bf16[2,39,8,128]{3,2,1,0:T(8,128)(2,1)S(1)}, bf16[2,39,8,128]{3,2,1,0:T(8,128)(2,1)S(1)}, u32[]{:S(2)}, u32[]{:S(2)}) %collective-permute-start.9) | collective-permute-done | bytes 159776 | tf_op jit(solution)/shard_map/ppermute | solution.py:565
  77.6 0.1 collective-permute-done.10.refs_3_
  77.7 1.1 %collective-permute-done.11.refs_4_ = bf16[2,39,8,128]{3,2,1,0:T(8,128)(2,1)S(1)} collective-permute-done((bf16[2,39,8,128]{3,2,1,0:T(8,128)(2,1)S(1)}, bf16[2,39,8,128]{3,2,1,0:T(8,128)(2,1)S(1)}, u32[]{:S(2)}, u32[]{:S(2)}) %collective-permute-start.11) | collective-permute-done | bytes 159776 | tf_op jit(solution)/shard_map/ppermute | solution.py:565
  78.8 0.0 collective-permute-done.12.refs_5_
  78.8 3.5 %collective-permute-done.13.refs_6_ = bf16[2,39,8,128]{3,2,1,0:T(8,128)(2,1)S(1)} collective-permute-done((bf16[2,39,8,128]{3,2,1,0:T(8,128)(2,1)S(1)}, bf16[2,39,8,128]{3,2,1,0:T(8,128)(2,1)S(1)}, u32[]{:S(2)}, u32[]{:S(2)}) %collective-permute-start.13) | collective-permute-done | bytes 159776 | tf_op jit(solution)/shard_map/ppermute | solution.py:565
  82.3 0.1 forward.1
  82.4 0.6 collective-permute-start.14
  83.0 0.0 all-to-all-done.1.refs_0_
  83.0 1.3 %combine.1.ready_ref = f32[39,8,128]{2,1,0:T(8,128)S(1)} custom-call(f32[16]{0:T(128)S(1)} %copy-done, bf16[16,39,8,128]{3,2,1,0:T(8,128)(2,1)S(1)} %all-to-all-done.1.refs_0_), custom_call_target="tpu_custom_call" | custom-call | flops 10000000 | bytes 2000000 | tf_op jit(solution)/shard_map/combine/pallas_call | solution.py:505
  84.3 0.4 collective-permute-done.14.refs_1_
  84.7 2.1 %finish.1 = f32[39,8,256]{2,1,0:T(8,128)} custom-call(f32[16]{0:T(128)S(1)} %copy-done, f32[39,8,128]{2,1,0:T(8,128)S(1)} %combine.1.ready_ref, bf16[8,39,8,128]{3,2,1,0:T(8,128)(2,1)S(1)} %get-tuple-element.49.refs_0_, bf16[8,39,8,128]{3,2,1,0:T(8,128)(2,1)S(1)} %collective-permute-done.14.refs_1_), custom_call_target="tpu_custom_call" | custom-call | flops 10000000 | bytes 2000000 | tf_op jit(solution)/shard_map/finish/pallas_call | solution.py:517
  (6 shorter events, 0.0 us)
Async XLA Ops:
  4.7 30.3 %all-to-all-start = ((bf16[8,39,16,128]{3,2,1,0:T(8,128)(2,1)}), bf16[8,39,16,128]{3,2,1,0:T(8,128)(2,1)S(1)}, u32[]{:S(2)}, u32[]{:S(2)}) async-start(bf16[8,39,16,128]{3,2,1,0:T(8,128)(2,1)} %get-tuple-element.31), calls=%async_computation | async-start | bytes 2555904 | tf_op jit(solution)/shard_map/all_to_all | solution.py:543
  10.8 11.8 %copy-start.2 = (f32[39,16]{0,1:T(8,128)S(1)}, f32[39,16]{0,1:T(8,128)}, u32[]{:S(2)}) copy-start(f32[39,16]{0,1:T(8,128)} %param.13) | copy-start | bytes 7492
  10.8 11.8 %copy-start.3 = (bf16[8,39]{1,0:T(8,128)(2,1)S(1)}, bf16[8,39]{1,0:T(8,128)(2,1)}, u32[]{:S(2)}) copy-start(bf16[8,39]{1,0:T(8,128)(2,1)} %analysis_ref.1) | copy-start | bytes 1876
  10.8 11.8 %copy-start.4 = (bf16[39,8]{0,1:T(8,128)(2,1)S(1)}, bf16[39,8]{0,1:T(8,128)(2,1)}, u32[]{:S(2)}) copy-start(bf16[39,8]{0,1:T(8,128)(2,1)} %param.16) | copy-start | bytes 1876
  10.9 11.8 %copy-start.5 = (s32[39]{0:T(128)S(1)}, s32[39]{0:T(128)}, u32[]{:S(2)}) copy-start(s32[39]{0:T(128)} %refs_0_.1) | copy-start | bytes 472
  15.6 15.4 %collective-permute-start = (bf16[39,16,128]{2,1,0:T(8,128)(2,1)}, bf16[39,16,128]{2,1,0:T(8,128)(2,1)S(1)}, u32[]{:S(2)}, u32[]{:S(2)}) collective-permute-start(bf16[39,16,128]{2,1,0:T(8,128)(2,1)} %get-tuple-element.33), channel_id=1, source_target_pairs={{0,4},{1,5},{2,6},{3,7},{4,0},{5,1},{6,2},{7,3},{8,12},{9,13},{10,... | collective-permute-start | bytes 479240 | tf_op jit(solution)/shard_map/ppermute | solution.py:549
  16.8 16.2 %collective-permute-start.1 = (bf16[39,16,128]{2,1,0:T(8,128)(2,1)}, bf16[39,16,128]{2,1,0:T(8,128)(2,1)S(1)}, u32[]{:S(2)}, u32[]{:S(2)}) collective-permute-start(bf16[39,16,128]{2,1,0:T(8,128)(2,1)} %get-tuple-element.34), channel_id=1, source_target_pairs={{0,1},{1,2},{2,3},{3,0},{4,5},{5,6},{6,7},{7,4},{8,9},{9,10},{10,1... | collective-permute-start | bytes 479240 | tf_op jit(solution)/shard_map/ppermute | solution.py:549
  18.1 28.2 %collective-permute-start.2 = (bf16[39,16,128]{2,1,0:T(8,128)(2,1)}, bf16[39,16,128]{2,1,0:T(8,128)(2,1)S(1)}, u32[]{:S(2)}, u32[]{:S(2)}) collective-permute-start(bf16[39,16,128]{2,1,0:T(8,128)(2,1)} %get-tuple-element.35), channel_id=1, source_target_pairs={{0,3},{1,0},{2,1},{3,2},{4,7},{5,4},{6,5},{7,6},{8,11},{9,8},{10,9... | collective-permute-start | bytes 479240 | tf_op jit(solution)/shard_map/ppermute | solution.py:549
  19.7 26.6 %collective-permute-start.3 = (bf16[39,16,128]{2,1,0:T(8,128)(2,1)}, bf16[39,16,128]{2,1,0:T(8,128)(2,1)}, u32[]{:S(2)}, u32[]{:S(2)}) collective-permute-start(bf16[39,16,128]{2,1,0:T(8,128)(2,1)} %get-tuple-element.36), channel_id=1, source_target_pairs={{0,6},{1,7},{2,4},{3,5},{4,2},{5,3},{6,0},{7,1},{8,14},{9,15},{10,... | collective-permute-start | bytes 479240 | tf_op jit(solution)/shard_map/ppermute | solution.py:549
  21.4 24.9 %collective-permute-start.4 = (bf16[39,16,128]{2,1,0:T(8,128)(2,1)}, bf16[39,16,128]{2,1,0:T(8,128)(2,1)}, u32[]{:S(2)}, u32[]{:S(2)}) collective-permute-start(bf16[39,16,128]{2,1,0:T(8,128)(2,1)} %get-tuple-element.37), channel_id=1, source_target_pairs={{0,5},{1,6},{2,7},{3,4},{4,1},{5,2},{6,3},{7,0},{8,13},{9,14},{10,... | collective-permute-start | bytes 479240 | tf_op jit(solution)/shard_map/ppermute | solution.py:549
  31.1 15.3 %collective-permute-start.5 = (bf16[39,16,128]{2,1,0:T(8,128)(2,1)}, bf16[39,16,128]{2,1,0:T(8,128)(2,1)}, u32[]{:S(2)}, u32[]{:S(2)}) collective-permute-start(bf16[39,16,128]{2,1,0:T(8,128)(2,1)} %get-tuple-element.38), channel_id=1, source_target_pairs={{0,7},{1,4},{2,5},{3,6},{4,3},{5,0},{6,1},{7,2},{8,15},{9,12},{10,... | collective-permute-start | bytes 479240 | tf_op jit(solution)/shard_map/ppermute | solution.py:549
  33.0 13.4 %collective-permute-start.6 = (bf16[39,16,128]{2,1,0:T(8,128)(2,1)}, bf16[39,16,128]{2,1,0:T(8,128)(2,1)}, u32[]{:S(2)}, u32[]{:S(2)}) collective-permute-start(bf16[39,16,128]{2,1,0:T(8,128)(2,1)} %get-tuple-element.39), channel_id=1, source_target_pairs={{0,2},{1,3},{2,0},{3,1},{4,6},{5,7},{6,4},{7,5},{8,10},{9,11},{10,... | collective-permute-start | bytes 479240 | tf_op jit(solution)/shard_map/ppermute | solution.py:549
  37.5 8.9 %copy-start.1 = (bf16[39,16,128]{2,1,0:T(8,128)(2,1)S(1)}, bf16[39,16,128]{2,1,0:T(8,128)(2,1)}, u32[]{:S(2)}) copy-start(bf16[39,16,128]{2,1,0:T(8,128)(2,1)} %get-tuple-element.40.refs_7_) | copy-start | bytes 479236
  37.5 45.5 %all-to-all-start.1 = ((bf16[16,39,8,128]{3,2,1,0:T(8,128)(2,1)}), bf16[16,39,8,128]{3,2,1,0:T(8,128)(2,1)S(1)}, u32[]{:S(2)}, u32[]{:S(2)}) async-start(bf16[16,39,8,128]{3,2,1,0:T(8,128)(2,1)} %shard_map.92), calls=%async_computation.1 | async-start | bytes 2555904 | tf_op jit(solution)/shard_map/all_to_all | solution.py:543
  49.4 33.5 %copy-start = (f32[16]{0:T(128)S(1)}, f32[16]{0:T(128)}, u32[]{:S(2)}) copy-start(f32[16]{0:T(128)} %weights_ref.3) | copy-start | bytes 196
  49.5 20.2 %collective-permute-start.7 = (bf16[2,39,8,128]{3,2,1,0:T(8,128)(2,1)S(1)}, bf16[2,39,8,128]{3,2,1,0:T(8,128)(2,1)S(1)}, u32[]{:S(2)}, u32[]{:S(2)}) collective-permute-start(bf16[2,39,8,128]{3,2,1,0:T(8,128)(2,1)S(1)} %get-tuple-element.41), channel_id=1, source_target_pairs={{0,80},{8,88},{16,64},{24,72},{32,112},{40,120},{48,96},{56,104},{... | collective-permute-start | bytes 479240 | tf_op jit(solution)/shard_map/ppermute | solution.py:565
  54.8 16.2 %collective-permute-start.8 = (bf16[2,39,8,128]{3,2,1,0:T(8,128)(2,1)S(1)}, bf16[2,39,8,128]{3,2,1,0:T(8,128)(2,1)S(1)}, u32[]{:S(2)}, u32[]{:S(2)}) collective-permute-start(bf16[2,39,8,128]{3,2,1,0:T(8,128)(2,1)S(1)} %get-tuple-element.42), channel_id=1, source_target_pairs={{0,64},{8,72},{16,80},{24,88},{32,96},{40,104},{48,112},{56,120},{... | collective-permute-start | bytes 479240 | tf_op jit(solution)/shard_map/ppermute | solution.py:565
  55.1 22.5 %collective-permute-start.9 = (bf16[2,39,8,128]{3,2,1,0:T(8,128)(2,1)S(1)}, bf16[2,39,8,128]{3,2,1,0:T(8,128)(2,1)S(1)}, u32[]{:S(2)}, u32[]{:S(2)}) collective-permute-start(bf16[2,39,8,128]{3,2,1,0:T(8,128)(2,1)S(1)} %get-tuple-element.43), channel_id=1, source_target_pairs={{0,48},{8,56},{16,32},{24,40},{32,80},{40,88},{48,64},{56,72},{64,... | collective-permute-start | bytes 479240 | tf_op jit(solution)/shard_map/ppermute | solution.py:565
  56.3 21.4 %collective-permute-start.10 = (bf16[2,39,8,128]{3,2,1,0:T(8,128)(2,1)S(1)}, bf16[2,39,8,128]{3,2,1,0:T(8,128)(2,1)S(1)}, u32[]{:S(2)}, u32[]{:S(2)}) collective-permute-start(bf16[2,39,8,128]{3,2,1,0:T(8,128)(2,1)S(1)} %get-tuple-element.44), channel_id=1, source_target_pairs={{0,112},{8,120},{16,96},{24,104},{32,16},{40,24},{48,0},{56,8},{64... | collective-permute-start | bytes 479240 | tf_op jit(solution)/shard_map/ppermute | solution.py:565
  60.2 18.6 %collective-permute-start.11 = (bf16[2,39,8,128]{3,2,1,0:T(8,128)(2,1)S(1)}, bf16[2,39,8,128]{3,2,1,0:T(8,128)(2,1)S(1)}, u32[]{:S(2)}, u32[]{:S(2)}) collective-permute-start(bf16[2,39,8,128]{3,2,1,0:T(8,128)(2,1)S(1)} %get-tuple-element.45), channel_id=1, source_target_pairs={{0,32},{8,40},{16,48},{24,56},{32,64},{40,72},{48,80},{56,88},{64,... | collective-permute-start | bytes 479240 | tf_op jit(solution)/shard_map/ppermute | solution.py:565
  69.7 9.1 %collective-permute-start.12 = (bf16[2,39,8,128]{3,2,1,0:T(8,128)(2,1)S(1)}, bf16[2,39,8,128]{3,2,1,0:T(8,128)(2,1)S(1)}, u32[]{:S(2)}, u32[]{:S(2)}) collective-permute-start(bf16[2,39,8,128]{3,2,1,0:T(8,128)(2,1)S(1)} %get-tuple-element.46), channel_id=1, source_target_pairs={{0,96},{8,104},{16,112},{24,120},{32,0},{40,8},{48,16},{56,24},{64... | collective-permute-start | bytes 479240 | tf_op jit(solution)/shard_map/ppermute | solution.py:565
  71.0 11.3 %collective-permute-start.13 = (bf16[2,39,8,128]{3,2,1,0:T(8,128)(2,1)S(1)}, bf16[2,39,8,128]{3,2,1,0:T(8,128)(2,1)S(1)}, u32[]{:S(2)}, u32[]{:S(2)}) collective-permute-start(bf16[2,39,8,128]{3,2,1,0:T(8,128)(2,1)S(1)} %get-tuple-element.47), channel_id=1, source_target_pairs={{0,16},{8,24},{16,0},{24,8},{32,48},{40,56},{48,32},{56,40},{64,80... | collective-permute-start | bytes 479240 | tf_op jit(solution)/shard_map/ppermute | solution.py:565
  82.4 2.3 %collective-permute-start.14 = (bf16[8,39,8,128]{3,2,1,0:T(8,128)(2,1)S(1)}, bf16[8,39,8,128]{3,2,1,0:T(8,128)(2,1)S(1)}, u32[]{:S(2)}, u32[]{:S(2)}) collective-permute-start(bf16[8,39,8,128]{3,2,1,0:T(8,128)(2,1)S(1)} %get-tuple-element.50), channel_id=1, source_target_pairs={{0,8},{8,0},{16,24},{24,16},{32,40},{40,32},{48,56},{56,48},{64,72... | collective-permute-start | bytes 1916936 | tf_op jit(solution)/shard_map/ppermute | solution.py:569
